TPU v7x, 512 devices: a whole 4x8x8 slice. The times are simulated.
512 devices in a mesh: dp: 8 (over y), seq: 64 (over z, x, core).
Axes of the slice: x: 4, y: 8, z: 8, core: 2. Of those that a mesh axis runs over, the one named last changes fastest.
Arguments:
- mel_frames: bfloat16 [8, 16384, 128], P('dp', 'seq'), may hold values from -16 to 16
- positions: int32 [8, 8192], P('dp', 'seq'), may hold values from 0 to 16383, as said below
- conv_weight: bfloat16 [128, 3, 1280], replicated, may hold values from -0.3125 to 0.3125
- conv_bias: float32 [1280], replicated, may hold values from -3 to 3
- proj_weight: bfloat16 [1280, 2048], P('dp'), may hold values from -0.15625 to 0.15625
- proj_bias: float32 [2048], replicated, may hold values from -3 to 3
- cotangent: bfloat16 [8, 16384, 2048], P('dp', 'seq'), may hold values from -0.032958984 to 0.032958984
Outputs:
- merged: bfloat16 [8, 16384, 2048], P('dp', 'seq')
- grad_weight: float32 [128, 3, 1280], P('seq', None, 'dp')
Inputs may be any that keep to these rules, and one draw needn't show every extreme that they name: Within a recording the 8192 entries are distinct. Block b of the sequence is positions b * 256 to b * 256 + 255; the 128 tokens of one window put at most 4 entries into any one block, and in each recording one block receives exactly 4 from every window.
All inputs are finite; a program needn't handle non-finite values.
Results may differ from a plain program's by a relative error of at most 0.012.
Values may be sent and summed in bfloat16 or wider, within the bound.
A program may use at most 64 MiB of HBM per device.

v0:
```python
import jax
import jax.numpy as jnp
from jax import lax
from jax.sharding import PartitionSpec as P

SQRT_HALF = 0.7071067811865476
INV_SQRT_TWO_PI = 0.3989422804014327


def gelu_value(x):
    return x * 0.5 * (1.0 + lax.erf(x * SQRT_HALF))


def gelu_slope(x):
    return 0.5 * (1.0 + lax.erf(x * SQRT_HALF)) + x * INV_SQRT_TWO_PI * jnp.exp(-0.5 * x * x)


def body(mel_frames, positions, conv_weight, conv_bias, proj_weight, proj_bias, cotangent):
    frames = mel_frames[0]
    local_spots = positions[0]
    grads_in = cotangent[0]
    owner_count = lax.axis_size("seq")
    frame_count = frames.shape[0]
    tok_count = frame_count // 2
    rows_own = grads_in.shape[0]
    capacity = rows_own // owner_count
    tap_count = conv_weight.shape[1]
    channels = conv_weight.shape[2]
    padded = jnp.pad(frames, ((1, 1), (0, 0)))
    stacked = jnp.concatenate([padded[k : k + frame_count] for k in range(tap_count)], axis=1)
    kernel = jnp.transpose(conv_weight, (1, 0, 2)).reshape(-1, channels)
    pre_act = jnp.dot(stacked, kernel, preferred_element_type=jnp.float32) + conv_bias
    act_pairs = gelu_value(pre_act).reshape(tok_count, 2, channels)
    pooled = (0.5 * (act_pairs[:, 0, :] + act_pairs[:, 1, :])).astype(jnp.bfloat16)
    full_weight = lax.all_gather(proj_weight, "dp", axis=0, tiled=True)
    owner_index = local_spots // rows_own
    owner_row = local_spots % rows_own
    onehot = (owner_index[:, None] == jnp.arange(owner_count, dtype=jnp.int32)[None, :]).astype(
        jnp.int32
    )
    rank_before = jnp.cumsum(onehot, axis=0) - onehot
    slot_rank = jnp.sum(rank_before * onehot, axis=1)
    slot_index = owner_index * capacity + slot_rank
    dest_rows = (
        jnp.full((owner_count * capacity,), rows_own, jnp.int32).at[slot_index].set(owner_row)
    )
    dest_rows = dest_rows.reshape(owner_count, capacity)
    contract_last = (((1,), (1,)), ((), ()))
    projected = (
        jnp.dot(pooled, full_weight, preferred_element_type=jnp.float32) + proj_bias
    ).astype(jnp.bfloat16)
    outgoing = (
        jnp.zeros((owner_count * capacity, projected.shape[1]), jnp.bfloat16)
        .at[slot_index]
        .set(projected)
    )
    outgoing = outgoing.reshape(owner_count, capacity, -1)
    arrived, arrived_rows = (
        lax.all_to_all(outgoing, "seq", split_axis=0, concat_axis=0, tiled=True),
        lax.all_to_all(dest_rows, "seq", split_axis=0, concat_axis=0, tiled=True),
    )
    flat_rows = arrived_rows.reshape(-1)
    merged = (
        jnp.zeros_like(grads_in)
        .at[flat_rows]
        .set(arrived.reshape(flat_rows.shape[0], -1), mode="drop")
    )
    picked = jnp.take(grads_in, flat_rows, axis=0, mode="clip").reshape(owner_count, capacity, -1)
    returned = lax.all_to_all(picked, "seq", split_axis=0, concat_axis=0, tiled=True)
    grad_tokens = returned.reshape(owner_count * capacity, -1)[slot_index]
    grad_pooled = lax.dot_general(
        grad_tokens, full_weight, contract_last, preferred_element_type=jnp.float32
    ).astype(jnp.bfloat16)
    slopes = gelu_slope(pre_act).reshape(tok_count, 2, channels)
    grad_pre = (0.5 * grad_pooled.astype(jnp.float32)[:, None, :] * slopes).astype(jnp.bfloat16)
    grad_pre = grad_pre.reshape(frame_count, channels)
    contract_first = (((0,), (0,)), ((), ()))
    tap_terms = [
        lax.dot_general(
            padded[k : k + frame_count],
            grad_pre,
            contract_first,
            preferred_element_type=jnp.float32,
        )
        for k in range(tap_count)
    ]
    seq_share = lax.psum_scatter(
        jnp.stack(tap_terms, axis=1), "seq", scatter_dimension=0, tiled=True
    )
    grad_weight = lax.psum_scatter(seq_share, "dp", scatter_dimension=2, tiled=True)
    return (merged[None], grad_weight)


def solution(mesh):
    in_specs = (
        P("dp", "seq", None),
        P("dp", "seq"),
        P(),
        P(),
        P("dp", None),
        P(),
        P("dp", "seq", None),
    )
    out_specs = (P("dp", "seq", None), P("seq", None, "dp"))
    return jax.shard_map(body, mesh=mesh, in_specs=in_specs, out_specs=out_specs, check_vma=False)
```

profile of v0, /device:TPU:1, one launch (start us, length us, event | category | flops | bytes accessed | tf_op | source)
XLA Modules:
  0.0 373.2 jit_solution(8471840743982743471)
XLA Ops:
  7.2 0.7 all-gather.2.cloned.1.call-update
  7.9 0.7 and_select_fusion
  9.0 0.7 fusion.23
  9.7 1.0 scatter_custom_fusion
  10.8 24.0 %all_to_all.19 = s32[64,1,4]{2,1,0:T(1,128)S(1)} all-to-all(s32[64,1,4]{2,1,0:T(1,128)S(1)} %bitcast.73), channel_id=1, replica_groups=mesh['dp'=8,'seq'=64] {'seq'}, dimensions={0} | all-to-all | bytes 2048 | tf_op jit(solution)/shard_map/all_to_all | solution.py:60
  34.9 1.4 gather_fusion
  36.3 1.2 reshape.174
  37.5 4.9 %all-to-all-start.2 = ((bf16[64,4,2048]{2,1,0:T(4,128)(2,1)}), bf16[64,4,2048]{2,1,0:T(4,128)(2,1)S(1)}, u32[]{:S(2)}, u32[]{:S(2)}) async-start(bf16[64,4,2048]{2,1,0:T(4,128)(2,1)} %reshape.174), calls=%async_computation.2 | async-start | bytes 2097152 | tf_op jit(solution)/shard_map/all_to_all | solution.py:69
  42.5 28.1 %all-to-all-done.2 = bf16[64,4,2048]{2,1,0:T(4,128)(2,1)S(1)} async-done(((bf16[64,4,2048]{2,1,0:T(4,128)(2,1)}), bf16[64,4,2048]{2,1,0:T(4,128)(2,1)S(1)}, u32[]{:S(2)}, u32[]{:S(2)}) %all-to-all-start.2) | async-done | bytes 1048608 | tf_op jit(solution)/shard_map/all_to_all | solution.py:69
  70.8 0.9 gather_fusion.1
  71.8 10.8 %all-gather.2.cloned.1.call-done = bf16[1280,2048]{1,0:T(8,128)(2,1)} async-done(((bf16[160,2048]{1,0:T(8,128)(2,1)}), bf16[1280,2048]{1,0:T(8,128)(2,1)}) %all-gather.2.cloned.1.call-update) | async-done | bytes 5242896 | tf_op jit(solution)/shard_map/all_gather | solution.py:35
  82.6 4.3 %fusion.2 = f32[128,1280]{1,0:T(8,128)S(1)} fusion(bf16[128,2048]{1,0:T(8,128)(2,1)S(1)} %gather_fusion.1, bf16[1280,2048]{1,0:T(8,128)(2,1)} %all-gather.2.cloned.1.call-done), kind=kOutput, calls=%fused_computation.13 | convolution fusion | flops 671580160 | bytes 6422528 | tf_op jit(solution)/shard_map/dot_general | solution.py:71
  87.4 2.0 mul.83
  89.4 3.6 fusion.7
  93.0 2.1 reshape.171
  95.1 1.0 fusion.29
  96.1 4.2 %fusion = bf16[128,2048]{1,0:T(8,128)(2,1)} fusion(bf16[1280,2048]{1,0:T(8,128)(2,1)} %all-gather.2.cloned.1.call-done, f32[2048]{0:T(1024)S(1)} %copy-done.2, f32[128,1,1280]{2,1,0:T(1,128)S(1)} %get-tuple-element.5, f32[128,1,1280]{2,1,0:T(1,128)S(1)} %get-tuple-element.4), kind=kOutput, calls=%fused_computation.10 | convolution fusion | flops 672104448 | bytes 7086080 | tf_op jit(solution)/shard_map/dot_general | solution.py:50
  100.3 2.4 scatter_custom_fusion.1
  102.7 1.2 reshape.172
  103.9 11.0 %all-to-all-start.1 = ((bf16[64,4,2048]{2,1,0:T(4,128)(2,1)}), bf16[64,4,2048]{2,1,0:T(4,128)(2,1)S(1)}, u32[]{:S(2)}, u32[]{:S(2)}) async-start(bf16[64,4,2048]{2,1,0:T(4,128)(2,1)} %reshape.172), calls=%async_computation.1 | async-start | bytes 2097152 | tf_op jit(solution)/shard_map/all_to_all | solution.py:59
  115.8 1.4 pad_maximum_fusion
  117.3 1.3 dynamic-slice
  119.8 0.7 reduce.5
  120.6 197.7 %all-reduce.4.cloned.1.call-done = f32[128,3,1280]{2,0,1:T(8,128)} async-done(((f32[128,3,1280]{2,0,1:T(8,128)}), f32[128,3,1280]{2,0,1:T(8,128)}) %all-reduce.4.cloned.1.call-update) | async-done | bytes 1966096
  318.4 0.9 constant_dynamic-slice_fusion
  319.3 2.0 copy.20
  321.3 3.8 %reshape.219 = f32[1280,6]{1,0:T(8,128)} reshape(f32[1280,3,2]{2,1,0:T(4,128)} %bitcast.65) | data formatting | bytes 61440
  325.1 34.8 %reduce-scatter.5.cloned.1.call-done = f32[160,6]{1,0:T(8,128)} async-done(((f32[1280,6]{1,0:T(8,128)}), f32[160,6]{1,0:T(8,128)}) %reduce-scatter.5.cloned.1.call-update) | async-done | bytes 3856
  359.9 1.1 reshape.220
  361.0 0.8 copy.21
  361.7 1.1 reshape.212
  362.9 3.8 %scatter_custom_fusion.2 = bf16[256,2048]{1,0:T(8,128)(2,1)} fusion(s32[256]{0:T(256)S(1)} %bitcast.74, bf16[256,2048]{1,0:T(8,128)(2,1)} %reshape.212, bf16[]{:T(256)} %constant.25.clone.1), kind=kCustom, calls=%fused_computation.26 | custom fusion | bytes 1049088 | tf_op jit(solution)/shard_map/scatter | solution.py:66
  (30 shorter events, 3.0 us)
Async XLA Ops:
  7.2 27.8 %copy-start = (bf16[1,256,2048]{2,1,0:T(8,128)(2,1)S(1)}, bf16[1,256,2048]{2,1,0:T(8,128)(2,1)}, u32[]{:S(2)}) copy-start(bf16[1,256,2048]{2,1,0:T(8,128)(2,1)} %param.13) | copy-start | bytes 3145732
  7.2 75.4 %all-gather.2.cloned.1.call-start = ((), (), s32[]{:S(2)}) async-start(), calls=%async_computation.4 | async-start | bytes 5898240 | tf_op jit(solution)/shard_map/all_gather | solution.py:35
  37.5 4.9 %copy-start.1 = (bf16[1,256,128]{2,1,0:T(8,128)(2,1)S(1)}, bf16[1,256,128]{2,1,0:T(8,128)(2,1)}, u32[]{:S(2)}) copy-start(bf16[1,256,128]{2,1,0:T(8,128)(2,1)} %param.7) | copy-start | bytes 196612
  37.5 33.1 %all-to-all-start.2 = ((bf16[64,4,2048]{2,1,0:T(4,128)(2,1)}), bf16[64,4,2048]{2,1,0:T(4,128)(2,1)S(1)}, u32[]{:S(2)}, u32[]{:S(2)}) async-start(bf16[64,4,2048]{2,1,0:T(4,128)(2,1)} %reshape.174), calls=%async_computation.2 | async-start | bytes 2097152 | tf_op jit(solution)/shard_map/all_to_all | solution.py:69
  87.4 2.0 copy-start.3
  95.1 1.0 copy-start.2
  103.9 257.8 %all-to-all-start.1 = ((bf16[64,4,2048]{2,1,0:T(4,128)(2,1)}), bf16[64,4,2048]{2,1,0:T(4,128)(2,1)S(1)}, u32[]{:S(2)}, u32[]{:S(2)}) async-start(bf16[64,4,2048]{2,1,0:T(4,128)(2,1)} %reshape.172), calls=%async_computation.1 | async-start | bytes 2097152 | tf_op jit(solution)/shard_map/all_to_all | solution.py:59
  114.9 203.4 %all-reduce.4.cloned.1.call-start = ((), (), s32[]{:S(2)}) async-start(), calls=%async_computation.6 | async-start | bytes 3932160
  117.3 242.6 %reduce-scatter.5.cloned.1.call-start = ((), (), s32[]{:S(2)}) async-start(), calls=%async_computation.5 | async-start | bytes 737280
Sparse Core Ops, SparseCore 0:
  10.1 72.4 all-gather.1
  119.2 199.0 all-reduce.3
  325.2 34.6 reduce-scatter.4
where the time goes:
time: 378 us; the launch traced here: 373 us
  waiting for transfers between devices  272 us (72%)
  local copies, waits for them, and re-layouts  29.4 us (8%)
  blocking collectives  24 us (6%)
  starting transfers between devices  16 us (4%)
  between operations  14.6 us (4%)
  matrix products  12.9 us (3%)
  other arithmetic  3.93 us (1%)
    unnamed x5, waiting for transfers between devices  233 us
    all_to_all x1, waiting for transfers between devices, body(): lax.all_to_all(picked, 'seq', split_axis=0, concat_axis=0, tiled=True)  28.1 us
    all_to_all x1, blocking collectives, body(): lax.all_to_all(dest_rows, 'seq', split_axis=0, concat_axis=0, tiled=True)  24 us
    all_to_all x1, starting transfers between devices, body(): lax.all_to_all(outgoing, 'seq', split_axis=0, concat_axis=0, tiled=True)  11 us
    all_gather x1, waiting for transfers between devices, body(): full_weight = lax.all_gather(proj_weight, 'dp', axis=0, tiled=True)  10.8 us
    unnamed x14, local copies, waits for them, and re-layouts  9.77 us
  transfers between devices with their start and end apart: 5, of which 4 were waited for; matrix products, arithmetic and copies ran while one was open for 5% of the time, Pallas kernels for 0%

commit v1 on v0

v1 whole, which is shorter than its diff:
```python
import jax
import jax.numpy as jnp
from jax import lax
from jax.sharding import PartitionSpec as P

SQRT_HALF = 0.7071067811865476
INV_SQRT_TWO_PI = 0.3989422804014327


def body(mel_frames, positions, conv_weight, conv_bias, proj_weight, proj_bias, cotangent):
    frames = mel_frames[0]
    spots = positions[0]
    grads_in = cotangent[0]
    n_own = lax.axis_size("seq")
    n_dp = lax.axis_size("dp")
    frame_count, mels = frames.shape
    tok = frame_count // 2
    rows_own, feats = grads_in.shape
    cap = rows_own // n_own
    taps = conv_weight.shape[1]
    ch = conv_weight.shape[2]
    f32, bf16 = jnp.float32, jnp.bfloat16

    full_weight = lax.all_gather(proj_weight, "dp", axis=0, tiled=True)
    padded = jnp.pad(frames, ((1, 1), (0, 0)))
    pairs = padded.reshape(tok + 1, 2 * mels)
    windows = jnp.concatenate([pairs[:-1], pairs[1:]], axis=1)
    owner = spots // rows_own
    row = (spots % rows_own).astype(bf16)
    extra = jnp.concatenate([row[:, None] + 1, jnp.zeros((tok, mels - 1), bf16)], axis=1)
    payload = jnp.concatenate([windows, extra], axis=1)
    earlier = jnp.arange(tok)[None, :] < jnp.arange(tok)[:, None]
    rank = jnp.sum((owner[:, None] == owner[None, :]) & earlier, axis=1)
    slot = owner * cap + rank
    place = (jnp.arange(n_own * cap)[:, None] == slot[None, :]).astype(bf16)
    outgoing = jnp.dot(place, payload, preferred_element_type=f32).astype(bf16)
    arrived = lax.all_to_all(
        outgoing.reshape(n_own, cap, -1), "seq", split_axis=0, concat_axis=0, tiled=True
    ).reshape(n_own * cap, -1)
    arrived_row = arrived[:, 4 * mels].astype(jnp.int32) - 1
    pick = jnp.arange(rows_own)[:, None] == arrived_row[None, :]
    used = jnp.any(pick, axis=1)
    x = jnp.dot(pick.astype(bf16), arrived[:, : 4 * mels], preferred_element_type=f32).astype(bf16)
    kernel = jnp.transpose(conv_weight, (1, 0, 2)).reshape(taps * mels, ch)
    x0, x1 = x[:, : taps * mels], x[:, mels:]
    pre0 = jnp.dot(x0, kernel, preferred_element_type=f32) + conv_bias
    pre1 = jnp.dot(x1, kernel, preferred_element_type=f32) + conv_bias
    phi0 = 0.5 * (1.0 + lax.erf(pre0 * SQRT_HALF))
    phi1 = 0.5 * (1.0 + lax.erf(pre1 * SQRT_HALF))
    pooled = (0.5 * (pre0 * phi0 + pre1 * phi1)).astype(bf16)
    slope0 = phi0 + pre0 * INV_SQRT_TWO_PI * jnp.exp(-0.5 * pre0 * pre0)
    slope1 = phi1 + pre1 * INV_SQRT_TWO_PI * jnp.exp(-0.5 * pre1 * pre1)
    contract_last = (((1,), (1,)), ((), ()))
    grad_pooled = (
        lax.dot_general(grads_in, full_weight, contract_last, preferred_element_type=f32)
        .astype(bf16)
        .astype(f32)
    )
    g0 = (0.5 * grad_pooled * slope0).astype(bf16)
    g1 = (0.5 * grad_pooled * slope1).astype(bf16)
    contract_first = (((0,), (0,)), ((), ()))
    part = lax.dot_general(x0, g0, contract_first, preferred_element_type=f32) + lax.dot_general(
        x1, g1, contract_first, preferred_element_type=f32
    )
    part = part.astype(bf16).reshape(taps, n_own, mels // n_own, ch)
    part = jnp.transpose(part, (1, 2, 0, 3)).reshape(n_own, -1, ch)
    part = lax.all_to_all(part, "seq", split_axis=0, concat_axis=0, tiled=True)
    part = jnp.sum(part.astype(f32), axis=0).astype(bf16)
    part = jnp.transpose(part.reshape(-1, n_dp, ch // n_dp), (1, 0, 2))
    part = lax.all_to_all(part, "dp", split_axis=0, concat_axis=0, tiled=True)
    grad_weight = jnp.sum(part.astype(f32), axis=0).reshape(mels // n_own, taps, ch // n_dp)
    projected = jnp.dot(pooled, full_weight, preferred_element_type=f32) + proj_bias
    merged = jnp.where(used[:, None], projected, 0.0).astype(bf16)
    return (merged[None], grad_weight)


def solution(mesh):
    in_specs = (
        P("dp", "seq", None),
        P("dp", "seq"),
        P(),
        P(),
        P("dp", None),
        P(),
        P("dp", "seq", None),
    )
    out_specs = (P("dp", "seq", None), P("seq", None, "dp"))
    return jax.shard_map(body, mesh=mesh, in_specs=in_specs, out_specs=out_specs, check_vma=False)
```

time: 378 us -> 160 us (0.42)
  waiting for transfers between devices: 272 us -> 72.3 us
  local copies, waits for them, and re-layouts: 29.4 us -> 7.17 us
  blocking collectives: 24 us -> 28.8 us
  matrix products: 12.9 us -> 16.7 us
    unnamed x5 -> x1, waiting for transfers between devices: 233 us -> 0.68 us
    all_gather x1, waiting for transfers between devices: 10.8 us -> 37.6 us  [body(): full_weight = lax.all_gather(proj_weight, 'dp', axis=0, tiled=True)]
    unnamed x14 -> x15, local copies, waits for them, and re-layouts: 9.77 us -> 1.43 us
    scatter x3 -> x0, local copies, waits for them, and re-layouts: 7.18 us -> none  [the longest x1 3.81 us: body(): merged = jnp.zeros_like(grads_in).at[flat_rows].set(arrived.reshape(flat_...]
    all_to_all x2, waiting for transfers between devices: 28.1 us -> 34 us  [the longest x1 33.5 us: body(): part = lax.all_to_all(part, 'seq', split_axis=0, concat_axis=0, tiled=True)]
    all_to_all x1, blocking collectives: 24 us -> 28.8 us  [body(): lax.all_to_all(outgoing.reshape(n_own, cap, -1), 'seq', split_axis=0, con...]
    dot_general x6 -> x8, matrix products: 12.9 us -> 16.7 us  [the longest x1 6.07 us: body(): jnp.dot(pooled, full_weight, preferred_element_type=f32) + proj_bias]
  transfers between devices with their start and end apart: 5 -> 3, of which waited for: 4 -> 3; matrix products, arithmetic and copies ran while one was open for 5% -> 9% of each run, Pallas kernels for 0% -> 0%
where the time goes in v1:
time: 160 us; the launch traced here: 158 us
  waiting for transfers between devices  72.3 us (45%)
  blocking collectives  28.8 us (18%)
  matrix products  16.7 us (10%)
  starting transfers between devices  15.2 us (10%)
  between operations  14.2 us (9%)
  local copies, waits for them, and re-layouts  7.17 us (4%)
  other arithmetic  3.37 us (2%)
    all_gather x1, waiting for transfers between devices, body(): full_weight = lax.all_gather(proj_weight, 'dp', axis=0, tiled=True)  37.6 us
    all_to_all x1, waiting for transfers between devices, body(): part = lax.all_to_all(part, 'seq', split_axis=0, concat_axis=0, tiled=True)  33.5 us
    all_to_all x1, blocking collectives, body(): lax.all_to_all(outgoing.reshape(n_own, cap, -1), 'seq', split_axis=0, con...  28.8 us
    all_to_all x1, starting transfers between devices, body(): part = lax.all_to_all(part, 'seq', split_axis=0, concat_axis=0, tiled=True)  11 us
    dot_general x1, matrix products, body(): jnp.dot(pooled, full_weight, preferred_element_type=f32) + proj_bias  6.07 us
    all_to_all x1, starting transfers between devices, body(): part = lax.all_to_all(part, 'dp', split_axis=0, concat_axis=0, tiled=True)  4.18 us
    dot_general x1, matrix products, body(): lax.dot_general(grads_in, full_weight, contract_last, preferred_element_t...  4.15 us
  transfers between devices with their start and end apart: 3, of which 3 were waited for; matrix products, arithmetic and copies ran while one was open for 9% of the time, Pallas kernels for 0%

profile of v1, /device:TPU:1, one launch (start us, length us, event | category | flops | bytes accessed | tf_op | source)
XLA Modules:
  0.0 157.8 jit_solution(6590703125307992225)
XLA Ops:
  7.2 0.7 all-gather.2.cloned.1.call-update
  7.9 0.7 fusion.42
  8.6 0.1 copy.26
  8.7 1.0 pad_slice_fusion.1
  9.8 0.7 fusion.55
  10.5 0.7 and_select_fusion.1
  11.2 0.2 convert_reduce_fusion.1
  11.3 0.7 fusion.44
  12.0 0.2 convolution_convert_fusion.1
  12.4 28.8 %all_to_all.15 = bf16[64,4,640]{2,1,0:T(4,128)(2,1)S(1)} all-to-all(bf16[64,4,640]{2,1,0:T(4,128)(2,1)S(1)} %reshape.128), channel_id=1, replica_groups=mesh['dp'=8,'seq'=64] {'seq'}, dimensions={0} | all-to-all | bytes 655360 | tf_op jit(solution)/shard_map/all_to_all | solution.py:37
  41.3 0.1 add_reduce_fusion
  41.4 0.2 convolution_convert_fusion.2
  41.6 1.8 %convolution_add_fusion.1 = f32[256,1280]{1,0:T(8,128)S(1)} fusion(bf16[384,1280]{1,0:T(8,128)(2,1)} %bitcast.35, f32[1280]{0:T(1024)S(1)} %copy-done.4, bf16[256,512]{1,0:T(8,128)(2,1)S(1)} %convolution_convert_fusion.2), kind=kOutput, calls=%fused_computation.1 | convolution fusion | flops 251985920 | bytes 2498560 | tf_op jit(solution)/shard_map/dot_general | solution.py:47
  43.4 1.6 convolution_add_fusion.2
  45.0 37.6 %all-gather.2.cloned.1.call-done = bf16[1280,2048]{1,0:T(8,128)(2,1)} async-done(((bf16[160,2048]{1,0:T(8,128)(2,1)}), bf16[1280,2048]{1,0:T(8,128)(2,1)}) %all-gather.2.cloned.1.call-update) | async-done | bytes 5242896 | tf_op jit(solution)/shard_map/all_gather | solution.py:24
  82.6 4.2 %fusion.4 = f32[256,1280]{1,0:T(8,128)S(1)} fusion(bf16[1280,2048]{1,0:T(8,128)(2,1)} %all-gather.2.cloned.1.call-done, bf16[1,256,2048]{2,1,0:T(8,128)(2,1)S(1)} %copy-done), kind=kOutput, calls=%fused_computation.9 | convolution fusion | flops 1343160320 | bytes 7602176 | tf_op jit(solution)/shard_map/dot_general | solution.py:55
  86.8 0.8 fusion.18
  87.6 1.8 %fusion = bf16[384,1280]{1,0:T(8,128)(2,1)} fusion(f32[384,1280]{1,0:T(8,128)S(1)} %fusion.18, f32[256,1280]{1,0:T(8,128)S(1)} %fusion.4, f32[256,1280]{1,0:T(8,128)S(1)} %convolution_add_fusion.1, bf16[256,512]{1,0:T(8,128)(2,1)S(1)} %convolution_convert_fusion.2), kind=kOutput, calls=%fused_computation.3 | convolution fusion | flops 255918080 | bytes 5767168 | tf_op jit(solution)/shard_map/dot_general | solution.py:62
  89.4 2.4 %reshape.131 = bf16[3,64,2,1280]{3,2,1,0:T(2,128)(2,1)S(1)} reshape(bf16[384,1280]{1,0:T(8,128)(2,1)} %fusion) | data formatting | bytes 1966080 | tf_op jit(solution)/shard_map/reshape | solution.py:65
  91.8 0.1 copy.27
  92.0 1.7 %copy.28 = bf16[64,6,1280]{2,1,0:T(8,128)(2,1)} copy(bf16[64,6,1280]{2,0,1:T(8,128)(2,1)S(1)} %bitcast.37) | data formatting | bytes 1966080 | tf_op jit(solution)/shard_map/reshape | solution.py:66
  93.7 11.0 %all-to-all-start.1 = ((bf16[64,6,1280]{2,1,0:T(8,128)(2,1)}), bf16[64,6,1280]{2,1,0:T(8,128)(2,1)S(1)}, u32[]{:S(2)}, u32[]{:S(2)}) async-start(bf16[64,6,1280]{2,1,0:T(8,128)(2,1)} %copy.28), calls=%async_computation.1 | async-start | bytes 2621440 | tf_op jit(solution)/shard_map/all_to_all | solution.py:67
  104.7 0.1 fusion.26
  104.8 33.5 %all-to-all-done.1 = bf16[64,6,1280]{2,1,0:T(8,128)(2,1)S(1)} async-done(((bf16[64,6,1280]{2,1,0:T(8,128)(2,1)}), bf16[64,6,1280]{2,1,0:T(8,128)(2,1)S(1)}, u32[]{:S(2)}, u32[]{:S(2)}) %all-to-all-start.1) | async-done | bytes 983072 | tf_op jit(solution)/shard_map/all_to_all | solution.py:67
  138.3 0.3 reduce_sum.34
  138.6 0.1 reshape.133
  138.7 0.7 reshape.136
  139.4 4.2 %all-to-all-start.2 = ((bf16[8,2,480]{2,1,0:T(2,128)(2,1)}), bf16[8,2,480]{2,1,0:T(2,128)(2,1)S(1)}, u32[]{:S(2)}, u32[]{:S(2)}) async-start(bf16[8,2,480]{2,1,0:T(2,128)(2,1)} %reshape.136), calls=%async_computation.2 | async-start | bytes 32768 | tf_op jit(solution)/shard_map/all_to_all | solution.py:70
  143.6 6.1 %fusion.5 = bf16[1,256,2048]{2,1,0:T(8,128)(2,1)} fusion(bf16[1280,2048]{1,0:T(8,128)(2,1)} %all-gather.2.cloned.1.call-done, f32[2048]{0:T(1024)S(1)} %copy-done.5, pred[256]{0:T(512)(128)(4,1)S(1)} %fusion.26, f32[256,1280]{1,0:T(8,128)} %copy-done.1, f32[256,1280]{1,0:T(8,128)} %convolution_add_fusion.2), kind=kOutput, calls=%fused_computation.10 | convolution fusion | flops 1347354624 | bytes 8921344 | tf_op jit(solution)/shard_map/dot_general | solution.py:72
  149.7 0.5 all-to-all-done.2
  150.2 0.1 reshape.137
  150.4 0.6 copy.30
  (22 shorter events, 0.4 us)
Async XLA Ops:
  7.2 75.4 %copy-start = (bf16[1,256,2048]{2,1,0:T(8,128)(2,1)S(1)}, bf16[1,256,2048]{2,1,0:T(8,128)(2,1)}, u32[]{:S(2)}) copy-start(bf16[1,256,2048]{2,1,0:T(8,128)(2,1)} %param.13) | copy-start | bytes 3145732
  7.2 75.4 %all-gather.2.cloned.1.call-start = ((), (), s32[]{:S(2)}) async-start(), calls=%async_computation.3 | async-start | bytes 5898240 | tf_op jit(solution)/shard_map/all_gather | solution.py:24
  12.3 29.4 %copy-start.4 = (f32[1280]{0:T(1024)S(1)}, f32[1280]{0:T(1024)}, u32[]{:S(2)}) copy-start(f32[1280]{0:T(1024)} %param.10) | copy-start | bytes 15364
  41.6 1.8 %copy-start.3 = (bf16[128,3,1280]{2,0,1:T(8,128)(2,1)S(1)}, bf16[128,3,1280]{2,0,1:T(8,128)(2,1)}, u32[]{:S(2)}) copy-start(bf16[128,3,1280]{2,0,1:T(8,128)(2,1)} %param.9) | copy-start | bytes 2949124
  43.4 44.2 %copy-start.1 = (f32[256,1280]{1,0:T(8,128)}, f32[256,1280]{1,0:T(8,128)S(1)}, u32[]{:S(2)}) copy-start(f32[256,1280]{1,0:T(8,128)S(1)} %convolution_add_fusion.1) | copy-start | bytes 3932164
  82.6 4.2 %copy-start.2 = (f32[256,1280]{1,0:T(8,128)S(1)}, f32[256,1280]{1,0:T(8,128)}, u32[]{:S(2)}) copy-start(f32[256,1280]{1,0:T(8,128)} %convolution_add_fusion.2) | copy-start | bytes 3932164
  93.7 44.6 %all-to-all-start.1 = ((bf16[64,6,1280]{2,1,0:T(8,128)(2,1)}), bf16[64,6,1280]{2,1,0:T(8,128)(2,1)S(1)}, u32[]{:S(2)}, u32[]{:S(2)}) async-start(bf16[64,6,1280]{2,1,0:T(8,128)(2,1)} %copy.28), calls=%async_computation.1 | async-start | bytes 2621440 | tf_op jit(solution)/shard_map/all_to_all | solution.py:67
  104.7 38.9 %copy-start.5 = (f32[2048]{0:T(1024)S(1)}, f32[2048]{0:T(1024)}, u32[]{:S(2)}) copy-start(f32[2048]{0:T(1024)} %param.12) | copy-start | bytes 24580
  139.4 10.8 %all-to-all-start.2 = ((bf16[8,2,480]{2,1,0:T(2,128)(2,1)}), bf16[8,2,480]{2,1,0:T(2,128)(2,1)S(1)}, u32[]{:S(2)}, u32[]{:S(2)}) async-start(bf16[8,2,480]{2,1,0:T(2,128)(2,1)} %reshape.136), calls=%async_computation.2 | async-start | bytes 32768 | tf_op jit(solution)/shard_map/all_to_all | solution.py:70
Sparse Core Ops, SparseCore 0:
  10.1 72.4 all-gather.1

commit v2 on v1

v2 whole, which is shorter than its diff:
```python
import functools

import jax
import jax.numpy as jnp
from jax import lax
from jax.experimental import pallas as pl
from jax.experimental.pallas import tpu as pltpu
from jax.sharding import PartitionSpec as P

SQRT_HALF = 0.7071067811865476
INV_SQRT_TWO_PI = 0.3989422804014327
F32, BF16, I32 = jnp.float32, jnp.bfloat16, jnp.int32
MESH = pl.DeviceIdType.MESH
NT = (((1,), (1,)), ((), ()))
NX, NC = 4, 2


def mo(value, k):
    return pl.multiple_of(value, k)


def kernel(
    ny,
    ns,
    nx,
    mel_ref,
    pos_ref,
    kt_ref,
    bias_ref,
    w_ref,
    pbias_ref,
    cot_ref,
    merged_ref,
    gw_ref,
    wf,
    cot2,
    kt,
    biast,
    msgs,
    arr,
    posv,
    fr,
    xt,
    pt,
    pts,
    ptr,
    slope,
    gt,
    zsend,
    zrecv,
    ysend,
    yrecv,
    xsend,
    xrecv,
    mscr,
    ring_send,
    ring_recv,
    sib_send,
    sib_recv,
    pos_sem,
    msg_sem,
    cot_sem,
    fr_sem,
    pt_sem,
    z_sem,
    y_sem,
    x_sem,
    loc_sem,
):
    nq = nx * NC
    nz = ns // nq
    frames, mels = mel_ref.shape
    tok = frames // 2
    rows = cot_ref.shape[0]
    feats = wf.shape[1]
    ch = wf.shape[0]
    shard = ch // ny
    half = shard // NC
    lp = gt.shape[0] // 2
    cap = rows // ns
    mr = 4 * cap
    km = kt.shape[1]
    taps = km // mels
    mz = mels // nz
    zr = km // nz
    mper = mels // ns

    y = lax.axis_index("dp")
    s = lax.axis_index("seq")
    c = lax.rem(s, NC)
    q = lax.rem(s, nq)
    z = s // nq
    sib = s + 1 - 2 * c
    up, down = lax.rem(y + 1, ny), lax.rem(y + ny - 1, ny)

    def remote(src, dst, ssem, rsem, dev):
        return pltpu.make_async_remote_copy(
            src_ref=src, dst_ref=dst, send_sem=ssem, recv_sem=rsem, device_id=dev, device_id_type=MESH
        )

    def drain(ref, sem):
        pltpu.make_async_copy(ref, ref, sem).wait()

    barrier = pltpu.get_barrier_semaphore()

    def hail_seq(i, carry):
        pl.semaphore_signal(barrier, inc=1, device_id=(y, lax.rem(s + i, ns)), device_id_type=MESH)
        return carry

    def hail_dp(i, carry):
        pl.semaphore_signal(barrier, inc=1, device_id=(lax.rem(y + i, ny), s), device_id_type=MESH)
        return carry

    lax.fori_loop(1, ny, hail_dp, 0)
    lax.fori_loop(1, ns, hail_seq, 0)

    own_w = pltpu.make_async_copy(w_ref, wf.at[pl.ds(mo(y * shard, 16), shard)], loc_sem.at[0])
    own_w.start()
    own_cot = pltpu.make_async_copy(cot_ref, cot2.at[pl.ds(0, rows)], loc_sem.at[1])
    own_cot.start()
    own_kt = pltpu.make_async_copy(kt_ref, kt, loc_sem.at[2])
    own_kt.start()

    before = (
        lax.broadcasted_iota(I32, (tok, tok), 0) < lax.broadcasted_iota(I32, (tok, tok), 1)
    ).astype(BF16)
    total = ns * mr

    def spread(hit, value):
        hit_b = hit.astype(F32).astype(BF16)
        rank = jnp.dot(hit_b, before, preferred_element_type=F32)
        lane = lax.broadcasted_iota(I32, (ns, 128), 1)
        table = jnp.zeros((ns, 128), F32)
        for k in range(cap):
            entry = jnp.sum(jnp.where(hit & (rank == k), value + 1.0, 0.0), axis=1, keepdims=True)
            table = table + jnp.where(lane == k, entry, 0.0)
        group = lax.broadcasted_iota(I32, (total, ns), 0) // mr
        expand = (group == lax.broadcasted_iota(I32, (total, ns), 1)).astype(F32).astype(BF16)
        wide = jnp.dot(expand, table.astype(BF16), preferred_element_type=F32)
        n = lax.broadcasted_iota(I32, (total, 128), 0)
        chosen = lax.broadcasted_iota(I32, (total, 128), 1) == lax.rem(n // 4, cap)
        return jnp.sum(jnp.where(chosen, wide, 0.0), axis=1, keepdims=True)

    pos_row = jnp.broadcast_to(pos_ref[...], (ns, tok))
    to_dest = (pos_row // rows) == lax.broadcasted_iota(I32, (ns, tok), 0)
    token = spread(to_dest, lax.broadcasted_iota(I32, (ns, tok), 1).astype(F32))
    n_col = lax.broadcasted_iota(I32, (total, 1), 0)
    f_col = lax.rem(n_col, 4).astype(F32)
    frame = jnp.where(token > 0.0, 2.0 * (token - 1.0) - 1.0 + f_col, -100.0)
    pick = (lax.broadcasted_iota(I32, (total, frames), 1).astype(F32) == frame).astype(F32)
    msgs[...] = jnp.dot(pick.astype(BF16), mel_ref[...], preferred_element_type=F32).astype(BF16)
    own_slot = pl.ds(mo(s * mr, 16), mr)
    arr[own_slot, :] = msgs[own_slot, :]
    posv[s] = pos_ref[...]

    for i in range(ch // 128):
        block = jnp.broadcast_to(bias_ref[:, 128 * i : 128 * (i + 1)], (128, 128))
        biast[128 * i : 128 * (i + 1), :] = jnp.transpose(block)
    gt[...] = jnp.zeros_like(gt)

    pl.semaphore_wait(barrier, ny + ns - 2)

    far = ny // 2
    cut = -(-(half // 2) // 16) * 16

    def wrows(owner, lo, size):
        return wf.at[pl.ds(mo(owner * shard + c * half + lo, 16), size)]

    def ring(step, way):
        owner = lax.rem(y + ny + 1 - step if way == 0 else y + step - 1, ny)
        if step < far:
            lo, size = 0, half
        else:
            lo, size = (0, cut) if way == 0 else (cut, half - cut)
        if step == 1:
            src = w_ref.at[pl.ds(mo(c * half + lo, 16), size)]
        else:
            src = wrows(owner, lo, size)
        target = (up, s) if way == 0 else (down, s)
        i = way * far + step - 1
        return remote(src, wrows(owner, lo, size), ring_send.at[i], ring_recv.at[i], target)

    def came(step, way):
        owner = lax.rem(y + ny - step if way == 0 else y + step, ny)
        if step < far:
            lo, size = 0, half
        else:
            lo, size = (0, cut) if way == 0 else (cut, half - cut)
        return wrows(owner, lo, size)

    def to_sibling(step, way):
        part = came(step, way)
        return remote(part, part, sib_send, sib_recv, (y, sib))

    def serve(step):
        for way in (0, 1):
            part = came(step, way)
            pltpu.make_async_copy(part, part, ring_recv.at[way * far + step - 1]).wait()
            if step < far:
                ring(step + 1, way).start()
            to_sibling(step, way).start()

    ring(1, 0).start()
    ring(1, 1).start()

    def post(i, carry):
        to = lax.rem(s + i, ns)
        remote(posv.at[s], posv.at[s], pos_sem.at[0], pos_sem.at[1], (y, to)).start()
        remote(
            msgs.at[pl.ds(mo(to * mr, 16), mr)],
            arr.at[pl.ds(mo(s * mr, 16), mr)],
            msg_sem.at[0],
            msg_sem.at[1],
            (y, to),
        ).start()
        return carry

    lax.fori_loop(1, ns, post, 0)
    send_cot = remote(
        cot_ref, cot2.at[pl.ds(rows, rows)], cot_sem.at[0], cot_sem.at[1], (y, sib)
    )
    send_cot.start()

    drain(posv.at[pl.ds(0, ns - 1)], pos_sem.at[1])
    all_pos = jnp.reshape(posv[...], (ns, tok))
    mine = (all_pos // rows) == s
    slot_row = spread(mine, lax.rem(all_pos, rows).astype(F32)) - 1.0
    row_lane = lax.broadcasted_iota(I32, (total, rows), 1).astype(F32)
    at_row = row_lane == slot_row
    n_f = lax.rem(lax.broadcasted_iota(I32, (total, rows), 0), 4)
    places = [(at_row & (n_f == f)).astype(F32).astype(BF16) for f in range(4)]
    used = lax.dot_general(
        places[0], jnp.ones((total, 128), BF16), (((0,), (0,)), ((), ())), preferred_element_type=F32
    )
    drain(arr.at[pl.ds(0, (ns - 1) * mr)], msg_sem.at[1])
    arr_t = jnp.transpose(arr[...])
    for f in range(4):
        fr[f, :, 0:rows] = jnp.dot(arr_t, places[f], preferred_element_type=F32).astype(BF16)
    send_fr = remote(
        fr.at[:, :, pl.ds(0, rows)], fr.at[:, :, pl.ds(rows, rows)], fr_sem.at[0], fr_sem.at[1], (y, sib)
    )
    send_fr.start()
    if far > 1:
        serve(1)
    own_kt.wait()
    send_fr.wait_recv()
    wide = 2 * rows
    for j in range(2):
        for zz in range(nz):
            for k in range(taps):
                at = zz * zr + k * mz
                xt[at : at + mz, j * wide : (j + 1) * wide] = fr[j + k, zz * mz : (zz + 1) * mz, :]

    def stem(yk, carry):
        r0 = mo(yk * shard + c * half, 16)
        l0 = mo(yk * half, 16)
        weights = kt[pl.ds(r0, half), :]
        b = biast[pl.ds(r0, half), :]
        for block in range(wide // 128):
            at = block * 128
            values, slopes = [], []
            for j in range(2):
                lanes = pl.ds(j * wide + at, 128)
                v = jnp.dot(weights, xt[:, lanes], preferred_element_type=F32) + b
                phi = 0.5 + 0.5 * lax.erf(v * SQRT_HALF)
                values.append(v * phi)
                slope[pl.ds(l0, half), lanes] = 0.5 * phi + v * (0.5 * INV_SQRT_TWO_PI) * jnp.exp(
                    -0.5 * v * v
                )
            pooled = (0.5 * (values[0] + values[1])).astype(BF16)
            if at < rows:
                pt[pl.ds(r0, half), at : at + 128] = pooled
            else:
                pts[pl.ds(l0, half), at - rows : at - rows + 128] = pooled
        remote(
            pts.at[pl.ds(l0, half)], ptr.at[pl.ds(l0, half)], pt_sem.at[0], pt_sem.at[1], (y, sib)
        ).start()
        return carry

    lax.fori_loop(0, ny, stem, 0)
    own_cot.wait()
    send_cot.wait_recv()
    own_w.wait()

    def back(owners):
        count = len(owners)
        w = jnp.concatenate([wrows(o, 0, half)[...] for o in owners], axis=0)
        gp = lax.dot_general(w, cot2[...], NT, preferred_element_type=F32).astype(BF16).astype(F32)
        for i, o in enumerate(owners):
            l0 = mo(o * half, 16)
            for j in range(2):
                lanes = slice(j * wide, (j + 1) * wide)
                g = gp[i * half : (i + 1) * half] * slope[pl.ds(l0, half), lanes]
                gt[i * lp : i * lp + half, lanes] = g.astype(BF16)
        part = lax.dot_general(
            xt[...], gt[0 : count * lp, :], NT, preferred_element_type=F32
        ).astype(BF16)
        for i, o in enumerate(owners):
            piece = part[:, i * lp : (i + 1) * lp]
            zsend[pl.ds(mo(o * km, 16), km), :] = piece
            own = zsend[pl.ds(mo(o * km + z * zr, 16), zr), :]
            zrecv[pl.ds(mo((o * nz + z) * zr, 16), zr), :] = own

            def pass_on(t, carry):
                zt = lax.rem(z + t, nz)
                remote(
                    zsend.at[pl.ds(mo(o * km + zt * zr, 16), zr)],
                    zrecv.at[pl.ds(mo((o * nz + z) * zr, 16), zr)],
                    z_sem.at[0],
                    z_sem.at[1],
                    (y, zt * nq + q),
                ).start()
                return carry

            lax.fori_loop(1, nz, pass_on, 0)

    back([y])
    for step in range(1, far + 1):
        if step > 1 or far == 1:
            serve(step)
        if step < far:
            back([lax.rem(y + ny - step, ny), lax.rem(y + step, ny)])
        else:
            back([lax.rem(y + far, ny)])

    drain(ptr, pt_sem.at[1])
    drain(wf.at[pl.ds(0, (ny - 1) * half)], sib_recv)
    o0 = 1 - c

    def place_pt(yk, carry):
        pt[pl.ds(mo(yk * shard + o0 * half, 16), half), :] = ptr[pl.ds(mo(yk * half, 16), half), :]
        return carry

    lax.fori_loop(0, ny, place_pt, 0)
    pooled_rows = jnp.transpose(pt[...])
    block_w = 512 if feats % 512 == 0 else feats
    keep = used[:, 0:1] > 0.0

    def project(i, carry):
        lanes = pl.ds(mo(i * block_w, 128), block_w)
        out = jnp.dot(pooled_rows, wf[:, lanes], preferred_element_type=F32) + pbias_ref[:, lanes]
        mscr[:, lanes] = jnp.where(keep, out, 0.0).astype(BF16)
        return carry

    lax.fori_loop(0, feats // block_w, project, 0)
    put = pltpu.make_async_copy(mscr, merged_ref, loc_sem.at[0])
    put.start()

    drain(zrecv.at[pl.ds(0, ny * (nz - 1) * zr)], z_sem.at[1])

    def sum_z(yk, carry):
        acc = jnp.zeros((zr, lp), F32)
        for i in range(nz):
            acc = acc + zrecv[pl.ds(mo((yk * nz + i) * zr, 16), zr), :].astype(F32)
        ysend[pl.ds(mo(yk * zr, 16), zr), :] = acc.astype(BF16)
        return carry

    lax.fori_loop(0, ny, sum_z, 0)
    yrecv[pl.ds(mo(y * zr, 16), zr), :] = ysend[pl.ds(mo(y * zr, 16), zr), :]

    def pass_y(i, carry):
        yt = lax.rem(y + i, ny)
        remote(
            ysend.at[pl.ds(mo(yt * zr, 16), zr)],
            yrecv.at[pl.ds(mo(y * zr, 16), zr)],
            y_sem.at[0],
            y_sem.at[1],
            (yt, s),
        ).start()
        return carry

    lax.fori_loop(1, ny, pass_y, 0)
    drain(yrecv.at[pl.ds(0, (ny - 1) * zr)], y_sem.at[1])
    acc = jnp.zeros((zr, lp), F32)
    for i in range(ny):
        acc = acc + yrecv[i * zr : (i + 1) * zr, :].astype(F32)
    xsend[...] = acc
    xrecv[pl.ds(mo(q * zr, 16), zr), :] = acc

    def pass_x(i, carry):
        remote(
            xsend,
            xrecv.at[pl.ds(mo(q * zr, 16), zr)],
            x_sem.at[0],
            x_sem.at[1],
            (y, z * nq + lax.rem(q + i, nq)),
        ).start()
        return carry

    lax.fori_loop(1, nq, pass_x, 0)
    drain(xrecv.at[pl.ds(0, (nq - 1) * zr)], x_sem.at[1])
    sums = []
    for h in range(NC):
        acc = jnp.zeros((zr, lp), F32)
        for i in range(nx):
            at = (i * NC + h) * zr
            acc = acc + xrecv[at : at + zr, :]
        sums.append(acc)
    line = lax.broadcasted_iota(I32, (zr, lp), 0)
    lane_pad = jnp.zeros((1, lp), F32)
    for m in range(mper):
        for k in range(taps):
            hit = line == k * mz + q * mper + m
            low = jnp.sum(jnp.where(hit, sums[0], 0.0), axis=0, keepdims=True)
            high = jnp.sum(jnp.where(hit, sums[1], 0.0), axis=0, keepdims=True)
            low = jnp.broadcast_to(jnp.concatenate([low, lane_pad], axis=1), (8, 2 * lp))
            high = jnp.broadcast_to(jnp.concatenate([high, lane_pad], axis=1), (8, 2 * lp))
            both = low + pltpu.roll(high, half, 1)
            gw_ref[m, k : k + 1, :] = both[0:1, :shard]

    for way in (0, 1):
        for step in range(1, far + 1):
            ring(step, way).wait_send()
    drain(wf.at[pl.ds(0, (ny - 1) * half)], sib_send)
    drain(posv.at[pl.ds(0, ns - 1)], pos_sem.at[0])
    drain(arr.at[pl.ds(0, (ns - 1) * mr)], msg_sem.at[0])
    send_cot.wait_send()
    send_fr.wait_send()
    drain(pts, pt_sem.at[0])
    drain(zrecv.at[pl.ds(0, ny * (nz - 1) * zr)], z_sem.at[0])
    drain(yrecv.at[pl.ds(0, (ny - 1) * zr)], y_sem.at[0])
    drain(xrecv.at[pl.ds(0, (nq - 1) * zr)], x_sem.at[0])
    put.wait()


def body(nx, mel_frames, positions, conv_weight, conv_bias, proj_weight, proj_bias, cotangent):
    ny, ns = lax.axis_size("dp"), lax.axis_size("seq")
    _, frames, mels = mel_frames.shape
    _, rows, feats = cotangent.shape
    taps, ch = conv_weight.shape[1:]
    tok = frames // 2
    nq = nx * NC
    nz = ns // nq
    km = taps * mels
    zr = km // nz
    half = ch // ny // NC
    lp = -(-half // 128) * 128
    far = ny // 2
    kt = jnp.transpose(conv_weight.reshape(nz, mels // nz, taps, ch), (3, 0, 2, 1)).reshape(ch, km)
    vmem = pl.BlockSpec(memory_space=pltpu.VMEM)
    hbm = pl.BlockSpec(memory_space=pl.ANY)
    total = 4 * rows
    dma = pltpu.SemaphoreType.DMA
    merged, gw = pl.pallas_call(
        functools.partial(kernel, ny, ns, nx),
        out_shape=(
            jax.ShapeDtypeStruct((rows, feats), BF16),
            jax.ShapeDtypeStruct((mels // ns, taps, ch // ny), F32),
        ),
        in_specs=[vmem, vmem, hbm, vmem, hbm, vmem, hbm],
        out_specs=(hbm, vmem),
        scratch_shapes=[
            pltpu.VMEM((ch, feats), BF16),
            pltpu.VMEM((2 * rows, feats), BF16),
            pltpu.VMEM((ch, km), BF16),
            pltpu.VMEM((ch, 128), F32),
            pltpu.VMEM((total, mels), BF16),
            pltpu.VMEM((total, mels), BF16),
            pltpu.VMEM((ns, 1, tok), I32),
            pltpu.VMEM((4, mels, 2 * rows), BF16),
            pltpu.VMEM((km, 4 * rows), BF16),
            pltpu.VMEM((ch, rows), BF16),
            pltpu.VMEM((ch // NC, rows), BF16),
            pltpu.VMEM((ch // NC, rows), BF16),
            pltpu.VMEM((ch // NC, 4 * rows), F32),
            pltpu.VMEM((2 * lp, 4 * rows), BF16),
            pltpu.VMEM((ny * km, lp), BF16),
            pltpu.VMEM((ny * nz * zr, lp), BF16),
            pltpu.VMEM((ny * zr, lp), BF16),
            pltpu.VMEM((ny * zr, lp), BF16),
            pltpu.VMEM((zr, lp), F32),
            pltpu.VMEM((nq * zr, lp), F32),
            pltpu.VMEM((rows, feats), BF16),
            dma((2 * far,)),
            dma((2 * far,)),
            dma,
            dma,
            dma((2,)),
            dma((2,)),
            dma((2,)),
            dma((2,)),
            dma((2,)),
            dma((2,)),
            dma((2,)),
            dma((2,)),
            dma((3,)),
        ],
        compiler_params=pltpu.CompilerParams(
            collective_id=0, has_side_effects=True, vmem_limit_bytes=48 << 20
        ),
    )(
        mel_frames[0],
        positions,
        kt,
        conv_bias[None],
        proj_weight,
        proj_bias[None],
        cotangent[0],
    )
    return (merged[None], gw)


def solution(mesh, nx=NX):
    in_specs = (
        P("dp", "seq", None),
        P("dp", "seq"),
        P(),
        P(),
        P("dp", None),
        P(),
        P("dp", "seq", None),
    )
    out_specs = (P("dp", "seq", None), P("seq", None, "dp"))
    return jax.shard_map(
        functools.partial(body, nx), mesh=mesh, in_specs=in_specs, out_specs=out_specs, check_vma=False
    )
```

time: 160 us -> 74.7 us (0.47); the launches traced: 158 us -> 74.5 us
  waiting for transfers between devices: 72.3 us -> 0 us
  Pallas kernels: 0 us -> 67.6 us
  blocking collectives: 28.8 us -> 0 us
  matrix products: 16.7 us -> 0 us
  starting transfers between devices: 15.2 us -> 0 us
  between operations: 14.2 us -> 0.7 us
  other arithmetic: 3.37 us -> 0 us
    pallas_call x0 -> x1, Pallas kernels: none -> 67.6 us  [body(): pl.pallas_call(functools.partial(kernel, ny, ns, nx), out_shape=(jax.Shap...]
    all_gather x1 -> x0, waiting for transfers between devices: 37.6 us -> none  [body(): full_weight = lax.all_gather(proj_weight, 'dp', axis=0, tiled=True)]
    all_to_all x2 -> x0, waiting for transfers between devices: 34 us -> none  [the longest x1 33.5 us: body(): part = lax.all_to_all(part, 'seq', split_axis=0, concat_axis=0, tiled=True)]
    all_to_all x1 -> x0, blocking collectives: 28.8 us -> none  [body(): lax.all_to_all(outgoing.reshape(n_own, cap, -1), 'seq', split_axis=0, con...]
    dot_general x8 -> x0, matrix products: 16.7 us -> none  [the longest x1 6.07 us: body(): jnp.dot(pooled, full_weight, preferred_element_type=f32) + proj_bias]
    all_to_all x2 -> x0, starting transfers between devices: 15.2 us -> none  [the longest x1 11 us: body(): part = lax.all_to_all(part, 'seq', split_axis=0, concat_axis=0, tiled=True)]
    reshape x7 -> x1, local copies, waits for them, and re-layouts: 4.5 us -> 1.7 us  [body(): jnp.transpose(conv_weight.reshape(nz, mels // nz, taps, ch), (3, 0, 2, 1))]
    transpose x1, local copies, waits for them, and re-layouts: 0.01 us -> 2.21 us  [body(): jnp.transpose(conv_weight.reshape(nz, mels // nz, taps, ch), (3, 0, 2, 1))]
  transfers between devices with their start and end apart: 3 -> 0, of which waited for: 3 -> 0; matrix products, arithmetic and copies ran while one was open for 9% -> 0% of each run, Pallas kernels for 0% -> 0%
where the time goes in v2:
time: 74.7 us; the launch traced here: 74.5 us
  Pallas kernels  67.6 us (90%)
  local copies, waits for them, and re-layouts  6.2 us (8%)
    pallas_call x1, Pallas kernels, body(): pl.pallas_call(functools.partial(kernel, ny, ns, nx), out_shape=(jax.Shap...  67.6 us
    transpose x1, local copies, waits for them, and re-layouts, body(): jnp.transpose(conv_weight.reshape(nz, mels // nz, taps, ch), (3, 0, 2, 1))  2.21 us
    reshape x1, local copies, waits for them, and re-layouts, body(): jnp.transpose(conv_weight.reshape(nz, mels // nz, taps, ch), (3, 0, 2, 1))  1.7 us
    unnamed x12, local copies, waits for them, and re-layouts  1.59 us

profile of v2, /device:TPU:1, one launch (start us, length us, event | category | flops | bytes accessed | tf_op | source)
XLA Modules:
  0.0 74.5 jit_solution(13237133162736034015)
XLA Ops:
  0.6 0.7 broadcast_in_dim.9.bias_ref
  1.3 2.2 %copy.13 = bf16[1280,8,3,16]{0,3,2,1:T(8,128)(2,1)} copy(bf16[1280,8,3,16]{0,3,1,2:T(8,128)(2,1)} %bitcast.13) | data formatting | bytes 1966080 | tf_op jit(solution)/shard_map/transpose | solution.py:439
  3.5 0.0 copy-start
  3.5 0.0 copy-start.1
  3.5 0.0 copy-start.2
  3.5 0.0 copy-start.3
  3.6 0.0 copy-start.4
  3.6 1.7 %copy.14.kt_ref = bf16[1280,384]{1,0:T(8,128)(2,1)S(1)} copy(bf16[1280,384]{0,1:T(8,128)(2,1)} %bitcast.12) | data formatting | bytes 1966080 | tf_op jit(solution)/shard_map/reshape | solution.py:439
  5.3 0.0 copy-done
  5.3 0.0 copy-done.1
  5.3 0.0 copy-done.2
  5.3 0.0 copy-done.3
  5.3 0.0 copy-done.4
  5.3 67.6 %shard_map.86 = (bf16[256,2048]{1,0:T(8,128)(2,1)S(1)}, f32[2,3,160]{2,1,0:T(4,128)S(1)}) custom-call(bf16[256,128]{1,0:T(8,128)(2,1)S(1)} %bitcast.10, s32[1,128]{1,0:T(1,128)S(1)} %copy-done.4, bf16[1280,384]{1,0:T(8,128)(2,1)S(1)} %copy.14.kt_ref, f32[1,1280]{1,0:T(1,128)S(1)} %broadcast_in_dim.9.bias_ref, bf16[160,2048]{1,0:T(8,128)(2,1)S(1)} %copy-done.1, ...), custom_call_target="tpu_custom_call" | custom-call | tf_op jit(solution)/shard_map/pallas_call | solution.py:444
  72.9 0.6 copy.15
  73.5 1.0 %copy.17 = bf16[1,256,2048]{2,1,0:T(8,128)(2,1)} copy(bf16[1,256,2048]{2,1,0:T(8,128)(2,1)S(1)} %bitcast.9) | data formatting | bytes 2097152
Async XLA Ops:
  3.5 1.7 %copy-start = (bf16[1,256,2048]{2,1,0:T(8,128)(2,1)S(1)}, bf16[1,256,2048]{2,1,0:T(8,128)(2,1)}, u32[]{:S(2)}) copy-start(bf16[1,256,2048]{2,1,0:T(8,128)(2,1)} %param.13) | copy-start | bytes 3145732
  3.5 1.7 %copy-start.1 = (bf16[160,2048]{1,0:T(8,128)(2,1)S(1)}, bf16[160,2048]{1,0:T(8,128)(2,1)}, u32[]{:S(2)}) copy-start(bf16[160,2048]{1,0:T(8,128)(2,1)} %w_ref.1) | copy-start | bytes 1966084
  3.5 1.7 %copy-start.2 = (bf16[1,256,128]{2,1,0:T(8,128)(2,1)S(1)}, bf16[1,256,128]{2,1,0:T(8,128)(2,1)}, u32[]{:S(2)}) copy-start(bf16[1,256,128]{2,1,0:T(8,128)(2,1)} %param.7) | copy-start | bytes 196612
  3.5 1.8 %copy-start.3 = (f32[2048]{0:T(1024)S(1)}, f32[2048]{0:T(1024)}, u32[]{:S(2)}) copy-start(f32[2048]{0:T(1024)} %param.12) | copy-start | bytes 24580
  3.6 1.8 %copy-start.4 = (s32[1,128]{1,0:T(1,128)S(1)}, s32[1,128]{1,0:T(1,128)}, u32[]{:S(2)}) copy-start(s32[1,128]{1,0:T(1,128)} %pos_ref.1) | copy-start | bytes 1540

commit v3 on v2

--- a/solution.py
+++ b/solution.py
@@ -19,13 +19,24 @@
     return pl.multiple_of(value, k)
 
 
+def steps_of(ny):
+    return {8: [[0, 1], [2], [3, 4]], 4: [[0, 1], [2]], 2: [[0], [1]]}[ny]
+
+
+def groups(ny):
+    far = ny // 2
+    return [
+        [o for t in steps for o in ([t] if t in (0, far) else [t, -t])] for steps in steps_of(ny)
+    ]
+
+
 def kernel(
     ny,
     ns,
     nx,
     mel_ref,
     pos_ref,
-    kt_ref,
+    cw_ref,
     bias_ref,
     w_ref,
     pbias_ref,
@@ -46,12 +57,12 @@
     ptr,
     slope,
     gt,
+    xsend,
+    xrecv,
     zsend,
     zrecv,
     ysend,
     yrecv,
-    xsend,
-    xrecv,
     mscr,
     ring_send,
     ring_recv,
@@ -62,9 +73,11 @@
     cot_sem,
     fr_sem,
     pt_sem,
+    x_send,
+    x_sem,
+    z_send,
     z_sem,
     y_sem,
-    x_sem,
     loc_sem,
 ):
     nq = nx * NC
@@ -76,20 +89,24 @@
     ch = wf.shape[0]
     shard = ch // ny
     half = shard // NC
-    lp = gt.shape[0] // 2
+    lanes_g = gt.shape[0]
     cap = rows // ns
     mr = 4 * cap
     km = kt.shape[1]
     taps = km // mels
-    mz = mels // nz
-    zr = km // nz
     mper = mels // ns
+    mc = NC * mper
+    xr = km // nx
+    mx = mels // nx
+    zr = taps * mc
+    zp = zrecv.shape[0] // (len(groups(ny)) * nz)
 
     y = lax.axis_index("dp")
     s = lax.axis_index("seq")
     c = lax.rem(s, NC)
     q = lax.rem(s, nq)
     z = s // nq
+    x = q // NC
     sib = s + 1 - 2 * c
     up, down = lax.rem(y + 1, ny), lax.rem(y + ny - 1, ny)
 
@@ -108,7 +125,9 @@
         return carry
 
     def hail_dp(i, carry):
-        pl.semaphore_signal(barrier, inc=1, device_id=(lax.rem(y + i, ny), s), device_id_type=MESH)
+        yt = lax.rem(y + i, ny)
+        pl.semaphore_signal(barrier, inc=1, device_id=(yt, s), device_id_type=MESH)
+        pl.semaphore_signal(barrier, inc=1, device_id=(yt, sib), device_id_type=MESH)
         return carry
 
     lax.fori_loop(1, ny, hail_dp, 0)
@@ -118,8 +137,6 @@
     own_w.start()
     own_cot = pltpu.make_async_copy(cot_ref, cot2.at[pl.ds(0, rows)], loc_sem.at[1])
     own_cot.start()
-    own_kt = pltpu.make_async_copy(kt_ref, kt, loc_sem.at[2])
-    own_kt.start()
 
     before = (
         lax.broadcasted_iota(I32, (tok, tok), 0) < lax.broadcasted_iota(I32, (tok, tok), 1)
@@ -148,17 +165,26 @@
     f_col = lax.rem(n_col, 4).astype(F32)
     frame = jnp.where(token > 0.0, 2.0 * (token - 1.0) - 1.0 + f_col, -100.0)
     pick = (lax.broadcasted_iota(I32, (total, frames), 1).astype(F32) == frame).astype(F32)
-    msgs[...] = jnp.dot(pick.astype(BF16), mel_ref[...], preferred_element_type=F32).astype(BF16)
+    p = lax.broadcasted_iota(I32, (mels, mels), 1)
+    from_m = lax.rem(p // mc, nz) * (nx * mc) + (p // mx) * mc + lax.rem(p, mc)
+    order = (lax.broadcasted_iota(I32, (mels, mels), 0) == from_m).astype(F32).astype(BF16)
+    mel_p = jnp.dot(mel_ref[...], order, preferred_element_type=F32).astype(BF16)
+    msgs[...] = jnp.dot(pick.astype(BF16), mel_p, preferred_element_type=F32).astype(BF16)
     own_slot = pl.ds(mo(s * mr, 16), mr)
     arr[own_slot, :] = msgs[own_slot, :]
     posv[s] = pos_ref[...]
 
+    for k in range(taps):
+        turned = jnp.transpose(cw_ref[k * mels : (k + 1) * mels, :])
+        kt[:, k * mels : (k + 1) * mels] = jnp.dot(
+            turned, order, preferred_element_type=F32
+        ).astype(BF16)
     for i in range(ch // 128):
-        block = jnp.broadcast_to(bias_ref[:, 128 * i : 128 * (i + 1)], (128, 128))
+        block = jnp.broadcast_to(bias_ref[128 * i : 128 * (i + 1)][None, :], (128, 128))
         biast[128 * i : 128 * (i + 1), :] = jnp.transpose(block)
     gt[...] = jnp.zeros_like(gt)
 
-    pl.semaphore_wait(barrier, ny + ns - 2)
+    pl.semaphore_wait(barrier, 2 * (ny - 1) + ns - 1)
 
     far = ny // 2
     cut = -(-(half // 2) // 16) * 16
@@ -204,7 +230,8 @@
     ring(1, 1).start()
 
     def post(i, carry):
-        to = lax.rem(s + i, ns)
+        hop = (i + 1) // 2
+        to = lax.rem(s + ns + hop * (2 * lax.rem(i, 2) - 1), ns)
         remote(posv.at[s], posv.at[s], pos_sem.at[0], pos_sem.at[1], (y, to)).start()
         remote(
             msgs.at[pl.ds(mo(to * mr, 16), mr)],
@@ -235,21 +262,22 @@
     drain(arr.at[pl.ds(0, (ns - 1) * mr)], msg_sem.at[1])
     arr_t = jnp.transpose(arr[...])
     for f in range(4):
-        fr[f, :, 0:rows] = jnp.dot(arr_t, places[f], preferred_element_type=F32).astype(BF16)
+        fr[f * mels : (f + 1) * mels, 0:rows] = jnp.dot(arr_t, places[f], preferred_element_type=F32).astype(BF16)
     send_fr = remote(
-        fr.at[:, :, pl.ds(0, rows)], fr.at[:, :, pl.ds(rows, rows)], fr_sem.at[0], fr_sem.at[1], (y, sib)
+        fr.at[:, pl.ds(0, rows)], fr.at[:, pl.ds(rows, rows)], fr_sem.at[0], fr_sem.at[1], (y, sib)
     )
     send_fr.start()
     if far > 1:
         serve(1)
-    own_kt.wait()
     send_fr.wait_recv()
     wide = 2 * rows
     for j in range(2):
-        for zz in range(nz):
+        for xx in range(nx):
             for k in range(taps):
-                at = zz * zr + k * mz
-                xt[at : at + mz, j * wide : (j + 1) * wide] = fr[j + k, zz * mz : (zz + 1) * mz, :]
+                at = xx * xr + k * mx
+                xt[at : at + mx, j * wide : (j + 1) * wide] = fr[
+                    (j + k) * mels + xx * mx : (j + k) * mels + (xx + 1) * mx, :
+                ]
 
     def stem(yk, carry):
         r0 = mo(yk * shard + c * half, 16)
@@ -261,7 +289,8 @@
             values, slopes = [], []
             for j in range(2):
                 lanes = pl.ds(j * wide + at, 128)
-                v = jnp.dot(weights, xt[:, lanes], preferred_element_type=F32) + b
+                window = fr[j * mels : j * mels + km, at : at + 128]
+                v = jnp.dot(weights, window, preferred_element_type=F32) + b
                 phi = 0.5 + 0.5 * lax.erf(v * SQRT_HALF)
                 values.append(v * phi)
                 slope[pl.ds(l0, half), lanes] = 0.5 * phi + v * (0.5 * INV_SQRT_TWO_PI) * jnp.exp(
@@ -282,46 +311,96 @@
     send_cot.wait_recv()
     own_w.wait()
 
-    def back(owners):
-        count = len(owners)
-        w = jnp.concatenate([wrows(o, 0, half)[...] for o in owners], axis=0)
+    def shard_at(offset):
+        return lax.rem(y + ny + offset, ny)
+
+    def back(g):
+        offsets = groups(ny)[g]
+        w = jnp.concatenate([wrows(shard_at(o), 0, half)[...] for o in offsets], axis=0)
         gp = lax.dot_general(w, cot2[...], NT, preferred_element_type=F32).astype(BF16).astype(F32)
-        for i, o in enumerate(owners):
-            l0 = mo(o * half, 16)
+        for i, o in enumerate(offsets):
+            l0 = mo(shard_at(o) * half, 16)
             for j in range(2):
                 lanes = slice(j * wide, (j + 1) * wide)
-                g = gp[i * half : (i + 1) * half] * slope[pl.ds(l0, half), lanes]
-                gt[i * lp : i * lp + half, lanes] = g.astype(BF16)
-        part = lax.dot_general(
-            xt[...], gt[0 : count * lp, :], NT, preferred_element_type=F32
+                grad = gp[i * half : (i + 1) * half] * slope[pl.ds(l0, half), lanes]
+                gt[i * half : (i + 1) * half, lanes] = grad.astype(BF16)
+        part = lax.dot_general(xt[...], gt[...], NT, preferred_element_type=F32)
+        xsend[g * km : (g + 1) * km, :] = part.astype(BF16)
+        mine_x = pl.ds(mo((g * nx + x) * xr, 16), xr)
+        xrecv[mine_x, :] = xsend[pl.ds(mo(g * km + x * xr, 16), xr), :]
+
+        def pass_x(t, carry):
+            to = lax.rem(x + t, nx)
+            remote(
+                xsend.at[pl.ds(mo(g * km + to * xr, 16), xr)],
+                xrecv.at[mine_x],
+                x_send.at[g],
+                x_sem.at[g],
+                (y, z * nq + to * NC + c),
+            ).start()
+            return carry
+
+        lax.fori_loop(1, nx, pass_x, 0)
+
+    n_new = lax.broadcasted_iota(I32, (nz * zp, xr), 0)
+    in_z = lax.rem(n_new, zp)
+    old = (in_z // mc) * mx + (n_new // zp) * mc + lax.rem(in_z, mc)
+    regroup = (
+        ((lax.broadcasted_iota(I32, (nz * zp, xr), 1) == old) & (in_z < zr)).astype(F32).astype(BF16)
+    )
+
+    def middle(g):
+        if nx > 1:
+            drain(xrecv.at[pl.ds(0, (nx - 1) * xr)], x_sem.at[g])
+        acc = jnp.zeros((xr, lanes_g), F32)
+        for i in range(nx):
+            acc = acc + xrecv[(g * nx + i) * xr : (g * nx + i + 1) * xr, :].astype(F32)
+        zsend[g * nz * zp : (g + 1) * nz * zp, :] = jnp.dot(
+            regroup, acc.astype(BF16), preferred_element_type=F32
         ).astype(BF16)
-        for i, o in enumerate(owners):
-            piece = part[:, i * lp : (i + 1) * lp]
-            zsend[pl.ds(mo(o * km, 16), km), :] = piece
-            own = zsend[pl.ds(mo(o * km + z * zr, 16), zr), :]
-            zrecv[pl.ds(mo((o * nz + z) * zr, 16), zr), :] = own
-
-            def pass_on(t, carry):
-                zt = lax.rem(z + t, nz)
-                remote(
-                    zsend.at[pl.ds(mo(o * km + zt * zr, 16), zr)],
-                    zrecv.at[pl.ds(mo((o * nz + z) * zr, 16), zr)],
-                    z_sem.at[0],
-                    z_sem.at[1],
-                    (y, zt * nq + q),
-                ).start()
-                return carry
-
-            lax.fori_loop(1, nz, pass_on, 0)
-
-    back([y])
-    for step in range(1, far + 1):
-        if step > 1 or far == 1:
-            serve(step)
-        if step < far:
-            back([lax.rem(y + ny - step, ny), lax.rem(y + step, ny)])
-        else:
-            back([lax.rem(y + far, ny)])
+        mine_z = pl.ds(mo((g * nz + z) * zp, 16), zp)
+        zrecv[mine_z, :] = zsend[mine_z, :]
+
+        def pass_z(t, carry):
+            hop = (t + 1) // 2
+            to = lax.rem(z + nz + hop * (2 * lax.rem(t, 2) - 1), nz)
+            remote(
+                zsend.at[pl.ds(mo((g * nz + to) * zp, 16), zp)],
+                zrecv.at[mine_z],
+                z_send.at[g],
+                z_sem.at[g],
+                (y, to * nq + q),
+            ).start()
+            return carry
+
+        lax.fori_loop(1, nz, pass_z, 0)
+
+    def last(g):
+        if nz > 1:
+            drain(zrecv.at[pl.ds(0, (nz - 1) * zp)], z_sem.at[g])
+        acc = jnp.zeros((zp, lanes_g), F32)
+        for i in range(nz):
+            acc = acc + zrecv[(g * nz + i) * zp : (g * nz + i + 1) * zp, :].astype(F32)
+        for i, o in enumerate(groups(ny)[g]):
+            turned = pltpu.roll(acc, lanes_g - i * half, 1) if i else acc
+            slot = (sum(len(h) for h in groups(ny)[:g]) + i) * zp
+            ysend[slot : slot + zp, :] = turned[:, : ysend.shape[1]].astype(BF16)
+            here = yrecv.at[pl.ds(mo((y * NC + c) * zp, 16), zp)]
+            piece = ysend.at[pl.ds(slot, zp)]
+            to = shard_at(o)
+            if o == 0:
+                yrecv[pl.ds(mo((y * NC + c) * zp, 16), zp), :] = ysend[slot : slot + zp, :]
+            else:
+                remote(piece, here, y_sem.at[0], y_sem.at[1], (to, s)).start()
+            remote(piece, here, y_sem.at[0], y_sem.at[1], (to, sib)).start()
+
+    for g, steps in enumerate(steps_of(ny)):
+        for step in steps:
+            if step > 1 or (step == 1 and far == 1):
+                serve(step)
+        back(g)
+        if g > 0:
+            middle(g - 1)
 
     drain(ptr, pt_sem.at[1])
     drain(wf.at[pl.ds(0, (ny - 1) * half)], sib_recv)
@@ -346,67 +425,27 @@
     put = pltpu.make_async_copy(mscr, merged_ref, loc_sem.at[0])
     put.start()
 
-    drain(zrecv.at[pl.ds(0, ny * (nz - 1) * zr)], z_sem.at[1])
-
-    def sum_z(yk, carry):
-        acc = jnp.zeros((zr, lp), F32)
-        for i in range(nz):
-            acc = acc + zrecv[pl.ds(mo((yk * nz + i) * zr, 16), zr), :].astype(F32)
-        ysend[pl.ds(mo(yk * zr, 16), zr), :] = acc.astype(BF16)
-        return carry
-
-    lax.fori_loop(0, ny, sum_z, 0)
-    yrecv[pl.ds(mo(y * zr, 16), zr), :] = ysend[pl.ds(mo(y * zr, 16), zr), :]
-
-    def pass_y(i, carry):
-        yt = lax.rem(y + i, ny)
-        remote(
-            ysend.at[pl.ds(mo(yt * zr, 16), zr)],
-            yrecv.at[pl.ds(mo(y * zr, 16), zr)],
-            y_sem.at[0],
-            y_sem.at[1],
-            (yt, s),
-        ).start()
-        return carry
-
-    lax.fori_loop(1, ny, pass_y, 0)
-    drain(yrecv.at[pl.ds(0, (ny - 1) * zr)], y_sem.at[1])
-    acc = jnp.zeros((zr, lp), F32)
-    for i in range(ny):
-        acc = acc + yrecv[i * zr : (i + 1) * zr, :].astype(F32)
-    xsend[...] = acc
-    xrecv[pl.ds(mo(q * zr, 16), zr), :] = acc
-
-    def pass_x(i, carry):
-        remote(
-            xsend,
-            xrecv.at[pl.ds(mo(q * zr, 16), zr)],
-            x_sem.at[0],
-            x_sem.at[1],
-            (y, z * nq + lax.rem(q + i, nq)),
-        ).start()
-        return carry
-
-    lax.fori_loop(1, nq, pass_x, 0)
-    drain(xrecv.at[pl.ds(0, (nq - 1) * zr)], x_sem.at[1])
+    middle(len(groups(ny)) - 1)
+    for g in range(len(groups(ny))):
+        last(g)
+    drain(yrecv.at[pl.ds(0, (ny * NC - 1) * zp)], y_sem.at[1])
     sums = []
     for h in range(NC):
-        acc = jnp.zeros((zr, lp), F32)
-        for i in range(nx):
-            at = (i * NC + h) * zr
-            acc = acc + xrecv[at : at + zr, :]
-        sums.append(acc)
-    line = lax.broadcasted_iota(I32, (zr, lp), 0)
-    lane_pad = jnp.zeros((1, lp), F32)
+        acc = jnp.zeros((zp, yrecv.shape[1]), F32)
+        for i in range(ny):
+            at = (i * NC + h) * zp
+            acc = acc + yrecv[at : at + zp, :].astype(F32)
+        pad = jnp.zeros((zp, lanes_g - acc.shape[1]), F32)
+        acc = jnp.concatenate([acc, pad], axis=1) if pad.shape[1] else acc
+        lane = lax.broadcasted_iota(I32, acc.shape, 1)
+        sums.append(jnp.where(lane < half, acc, 0.0))
+    both = sums[0] + pltpu.roll(sums[1], half, 1)
+    line = lax.broadcasted_iota(I32, both.shape, 0)
     for m in range(mper):
         for k in range(taps):
-            hit = line == k * mz + q * mper + m
-            low = jnp.sum(jnp.where(hit, sums[0], 0.0), axis=0, keepdims=True)
-            high = jnp.sum(jnp.where(hit, sums[1], 0.0), axis=0, keepdims=True)
-            low = jnp.broadcast_to(jnp.concatenate([low, lane_pad], axis=1), (8, 2 * lp))
-            high = jnp.broadcast_to(jnp.concatenate([high, lane_pad], axis=1), (8, 2 * lp))
-            both = low + pltpu.roll(high, half, 1)
-            gw_ref[m, k : k + 1, :] = both[0:1, :shard]
+            hit = line == k * mc + c * mper + m
+            one = jnp.sum(jnp.where(hit, both, 0.0), axis=0, keepdims=True)
+            gw_ref[k, m : m + 1, :] = one[:, :shard]
 
     for way in (0, 1):
         for step in range(1, far + 1):
@@ -417,9 +456,12 @@
     send_cot.wait_send()
     send_fr.wait_send()
     drain(pts, pt_sem.at[0])
-    drain(zrecv.at[pl.ds(0, ny * (nz - 1) * zr)], z_sem.at[0])
-    drain(yrecv.at[pl.ds(0, (ny - 1) * zr)], y_sem.at[0])
-    drain(xrecv.at[pl.ds(0, (nq - 1) * zr)], x_sem.at[0])
+    for g in range(len(groups(ny))):
+        if nx > 1:
+            drain(xrecv.at[pl.ds(0, (nx - 1) * xr)], x_send.at[g])
+        if nz > 1:
+            drain(zrecv.at[pl.ds(0, (nz - 1) * zp)], z_send.at[g])
+    drain(yrecv.at[pl.ds(0, (ny * NC - 1) * zp)], y_sem.at[0])
     put.wait()
 
 
@@ -432,11 +474,14 @@
     nq = nx * NC
     nz = ns // nq
     km = taps * mels
-    zr = km // nz
     half = ch // ny // NC
-    lp = -(-half // 128) * 128
     far = ny // 2
-    kt = jnp.transpose(conv_weight.reshape(nz, mels // nz, taps, ch), (3, 0, 2, 1)).reshape(ch, km)
+    n_groups = len(groups(ny))
+    lanes_g = -(-max(max(len(g) for g in groups(ny)) * half, ch // ny) // 128) * 128
+    lanes_y = -(-half // 128) * 128
+    xr = km // nx
+    zp = -(-taps * NC * (mels // ns) // 16) * 16
+    cw = jnp.transpose(conv_weight, (1, 0, 2)).reshape(km, ch)
     vmem = pl.BlockSpec(memory_space=pltpu.VMEM)
     hbm = pl.BlockSpec(memory_space=pl.ANY)
     total = 4 * rows
@@ -445,9 +490,9 @@
         functools.partial(kernel, ny, ns, nx),
         out_shape=(
             jax.ShapeDtypeStruct((rows, feats), BF16),
-            jax.ShapeDtypeStruct((mels // ns, taps, ch // ny), F32),
+            jax.ShapeDtypeStruct((taps, mels // ns, ch // ny), F32),
         ),
-        in_specs=[vmem, vmem, hbm, vmem, hbm, vmem, hbm],
+        in_specs=[vmem, vmem, vmem, vmem, hbm, vmem, hbm],
         out_specs=(hbm, vmem),
         scratch_shapes=[
             pltpu.VMEM((ch, feats), BF16),
@@ -457,19 +502,19 @@
             pltpu.VMEM((total, mels), BF16),
             pltpu.VMEM((total, mels), BF16),
             pltpu.VMEM((ns, 1, tok), I32),
-            pltpu.VMEM((4, mels, 2 * rows), BF16),
+            pltpu.VMEM((4 * mels, 2 * rows), BF16),
             pltpu.VMEM((km, 4 * rows), BF16),
             pltpu.VMEM((ch, rows), BF16),
             pltpu.VMEM((ch // NC, rows), BF16),
             pltpu.VMEM((ch // NC, rows), BF16),
             pltpu.VMEM((ch // NC, 4 * rows), F32),
-            pltpu.VMEM((2 * lp, 4 * rows), BF16),
-            pltpu.VMEM((ny * km, lp), BF16),
-            pltpu.VMEM((ny * nz * zr, lp), BF16),
-            pltpu.VMEM((ny * zr, lp), BF16),
-            pltpu.VMEM((ny * zr, lp), BF16),
-            pltpu.VMEM((zr, lp), F32),
-            pltpu.VMEM((nq * zr, lp), F32),
+            pltpu.VMEM((lanes_g, 4 * rows), BF16),
+            pltpu.VMEM((n_groups * km, lanes_g), BF16),
+            pltpu.VMEM((n_groups * km, lanes_g), BF16),
+            pltpu.VMEM((n_groups * nz * zp, lanes_g), BF16),
+            pltpu.VMEM((n_groups * nz * zp, lanes_g), BF16),
+            pltpu.VMEM((ny * zp, lanes_y), BF16),
+            pltpu.VMEM((ny * NC * zp, lanes_y), BF16),
             pltpu.VMEM((rows, feats), BF16),
             dma((2 * far,)),
             dma((2 * far,)),
@@ -480,10 +525,12 @@
             dma((2,)),
             dma((2,)),
             dma((2,)),
-            dma((2,)),
-            dma((2,)),
-            dma((2,)),
-            dma((3,)),
+            dma((n_groups,)),
+            dma((n_groups,)),
+            dma((n_groups,)),
+            dma((n_groups,)),
+            dma((2,)),
+            dma((2,)),
         ],
         compiler_params=pltpu.CompilerParams(
             collective_id=0, has_side_effects=True, vmem_limit_bytes=48 << 20
@@ -491,13 +538,13 @@
     )(
         mel_frames[0],
         positions,
-        kt,
-        conv_bias[None],
+        cw,
+        conv_bias,
         proj_weight,
         proj_bias[None],
         cotangent[0],
     )
-    return (merged[None], gw)
+    return (merged[None], jnp.transpose(gw, (1, 0, 2)))
 
 
 def solution(mesh, nx=NX):

time: 74.7 us -> 76 us (1.017)
  local copies, waits for them, and re-layouts: 6.2 us -> 7.96 us
    unnamed x12 -> x16, local copies, waits for them, and re-layouts: 1.59 us -> 7.96 us
    transpose x1 -> x0, local copies, waits for them, and re-layouts: 2.21 us -> none  [body(): jnp.transpose(conv_weight.reshape(nz, mels // nz, taps, ch), (3, 0, 2, 1))]
    reshape x1 -> x0, local copies, waits for them, and re-layouts: 1.7 us -> none  [body(): jnp.transpose(conv_weight.reshape(nz, mels // nz, taps, ch), (3, 0, 2, 1))]
where the time goes in v3:
time: 76 us; the launch traced here: 75.6 us
  Pallas kernels  67 us (88%)
  local copies, waits for them, and re-layouts  7.96 us (10%)
    pallas_call x1, Pallas kernels, body(): pl.pallas_call(functools.partial(kernel, ny, ns, nx), out_shape=(jax.Shap...  67 us
    unnamed x16, local copies, waits for them, and re-layouts  7.96 us

profile of v3, /device:TPU:1, one launch (start us, length us, event | category | flops | bytes accessed | tf_op | source)
XLA Modules:
  0.0 75.6 jit_solution(16750609403692334145)
XLA Ops:
  0.6 0.0 copy-start.6
  0.6 0.6 copy-done.6
  1.3 0.0 copy-start
  1.3 1.2 %copy-done = bf16[1,256,2048]{2,1,0:T(8,128)(2,1)S(1)} copy-done((bf16[1,256,2048]{2,1,0:T(8,128)(2,1)S(1)}, bf16[1,256,2048]{2,1,0:T(8,128)(2,1)}, u32[]{:S(2)}) %copy-start) | copy-done | bytes 1048600
  2.5 0.0 copy-start.1
  2.5 1.2 %copy-done.1 = bf16[128,3,1280]{2,0,1:T(8,128)(2,1)S(1)} copy-done((bf16[128,3,1280]{2,0,1:T(8,128)(2,1)S(1)}, bf16[128,3,1280]{2,0,1:T(8,128)(2,1)}, u32[]{:S(2)}) %copy-start.1) | copy-done | bytes 983064
  3.7 0.0 copy-start.2
  3.7 1.1 %copy-done.2 = bf16[160,2048]{1,0:T(8,128)(2,1)S(1)} copy-done((bf16[160,2048]{1,0:T(8,128)(2,1)S(1)}, bf16[160,2048]{1,0:T(8,128)(2,1)}, u32[]{:S(2)}) %copy-start.2) | copy-done | bytes 655384
  4.8 0.0 copy-start.3
  4.8 0.8 %copy-done.3 = bf16[1,256,128]{2,1,0:T(8,128)(2,1)S(1)} copy-done((bf16[1,256,128]{2,1,0:T(8,128)(2,1)S(1)}, bf16[1,256,128]{2,1,0:T(8,128)(2,1)}, u32[]{:S(2)}) %copy-start.3) | copy-done | bytes 65560
  5.6 0.0 copy-start.4
  5.6 0.7 copy-done.4
  6.3 0.0 copy-start.5
  6.3 0.7 copy-done.5
  7.0 67.0 %shard_map.86 = (bf16[256,2048]{1,0:T(8,128)(2,1)S(1)}, f32[3,2,160]{2,1,0:T(2,128)S(1)}) custom-call(bf16[256,128]{1,0:T(8,128)(2,1)S(1)} %bitcast.11, s32[1,128]{1,0:T(1,128)S(1)} %copy-done.6, bf16[384,1280]{1,0:T(8,128)(2,1)S(1)} %bitcast.10, f32[1280]{0:T(1024)S(1)} %copy-done.4, bf16[160,2048]{1,0:T(8,128)(2,1)S(1)} %copy-done.2, ...), custom_call_target="tpu_custom_call" | custom-call | tf_op jit(solution)/shard_map/pallas_call | solution.py:489
  74.0 1.0 %copy.11 = bf16[1,256,2048]{2,1,0:T(8,128)(2,1)} copy(bf16[1,256,2048]{2,1,0:T(8,128)(2,1)S(1)} %bitcast.9) | data formatting | bytes 2097152
  75.0 0.6 copy.12
Async XLA Ops:
  0.6 0.7 copy-start.6
  1.3 1.2 %copy-start = (bf16[1,256,2048]{2,1,0:T(8,128)(2,1)S(1)}, bf16[1,256,2048]{2,1,0:T(8,128)(2,1)}, u32[]{:S(2)}) copy-start(bf16[1,256,2048]{2,1,0:T(8,128)(2,1)} %param.13) | copy-start | bytes 3145732
  2.5 1.2 %copy-start.1 = (bf16[128,3,1280]{2,0,1:T(8,128)(2,1)S(1)}, bf16[128,3,1280]{2,0,1:T(8,128)(2,1)}, u32[]{:S(2)}) copy-start(bf16[128,3,1280]{2,0,1:T(8,128)(2,1)} %param.9) | copy-start | bytes 2949124
  3.7 1.1 %copy-start.2 = (bf16[160,2048]{1,0:T(8,128)(2,1)S(1)}, bf16[160,2048]{1,0:T(8,128)(2,1)}, u32[]{:S(2)}) copy-start(bf16[160,2048]{1,0:T(8,128)(2,1)} %w_ref.1) | copy-start | bytes 1966084
  4.8 0.8 %copy-start.3 = (bf16[1,256,128]{2,1,0:T(8,128)(2,1)S(1)}, bf16[1,256,128]{2,1,0:T(8,128)(2,1)}, u32[]{:S(2)}) copy-start(bf16[1,256,128]{2,1,0:T(8,128)(2,1)} %param.7) | copy-start | bytes 196612
  5.6 0.7 copy-start.4
  6.3 0.7 copy-start.5

commit v4 on v3

--- a/solution.py
+++ b/solution.py
@@ -34,15 +34,20 @@
     ny,
     ns,
     nx,
+    mel_in,
+    pos_in,
+    cw_in,
+    bias_in,
+    w_ref,
+    pbias_in,
+    cot_ref,
+    merged_ref,
+    gw_ref,
     mel_ref,
     pos_ref,
     cw_ref,
     bias_ref,
-    w_ref,
     pbias_ref,
-    cot_ref,
-    merged_ref,
-    gw_ref,
     wf,
     cot2,
     kt,
@@ -68,6 +73,8 @@
     ring_recv,
     sib_send,
     sib_recv,
+    share_send,
+    share_recv,
     pos_sem,
     msg_sem,
     cot_sem,
@@ -134,9 +141,25 @@
     lax.fori_loop(1, ns, hail_seq, 0)
 
     own_w = pltpu.make_async_copy(w_ref, wf.at[pl.ds(mo(y * shard, 16), shard)], loc_sem.at[0])
+    own_cot = pltpu.make_async_copy(cot_ref, cot2.at[pl.ds(0, rows)], loc_sem.at[1])
+    loads = [
+        pltpu.make_async_copy(src, dst, loc_sem.at[2 + i])
+        for i, (src, dst) in enumerate(
+            [
+                (pos_in, pos_ref),
+                (mel_in, mel_ref),
+                (cw_in, cw_ref),
+                (bias_in, bias_ref),
+                (pbias_in, pbias_ref),
+            ]
+        )
+    ]
+    for load in loads:
+        load.start()
     own_w.start()
-    own_cot = pltpu.make_async_copy(cot_ref, cot2.at[pl.ds(0, rows)], loc_sem.at[1])
     own_cot.start()
+    loads[0].wait()
+    loads[1].wait()
 
     before = (
         lax.broadcasted_iota(I32, (tok, tok), 0) < lax.broadcasted_iota(I32, (tok, tok), 1)
@@ -174,6 +197,8 @@
     arr[own_slot, :] = msgs[own_slot, :]
     posv[s] = pos_ref[...]
 
+    for load in loads[2:]:
+        load.wait()
     for k in range(taps):
         turned = jnp.transpose(cw_ref[k * mels : (k + 1) * mels, :])
         kt[:, k * mels : (k + 1) * mels] = jnp.dot(
@@ -184,50 +209,74 @@
         biast[128 * i : 128 * (i + 1), :] = jnp.transpose(block)
     gt[...] = jnp.zeros_like(gt)
 
+    own_w.wait()
     pl.semaphore_wait(barrier, 2 * (ny - 1) + ns - 1)
 
     far = ny // 2
     cut = -(-(half // 2) // 16) * 16
 
+    shared = feats // 2
+    part = shared // nx
+
     def wrows(owner, lo, size):
         return wf.at[pl.ds(mo(owner * shard + c * half + lo, 16), size)]
 
-    def ring(step, way):
+    def span(step, way):
+        if step < far:
+            return 0, half
+        return (0, cut) if way == 0 else (cut, half - cut)
+
+    def piece(owner, step, way, kind):
+        lo, size = span(step, way)
+        row = pl.ds(mo(owner * shard + c * half + lo, 16), size)
+        if kind == 0:
+            return wf.at[row, pl.ds(mo(shared + x * part, 128), part)]
+        return wf.at[row, pl.ds(0, shared)]
+
+    def ring_sem(step, way, kind):
+        return (way * far + step - 1) * 2 + kind
+
+    def ring(step, way, kind):
         owner = lax.rem(y + ny + 1 - step if way == 0 else y + step - 1, ny)
-        if step < far:
-            lo, size = 0, half
-        else:
-            lo, size = (0, cut) if way == 0 else (cut, half - cut)
-        if step == 1:
-            src = w_ref.at[pl.ds(mo(c * half + lo, 16), size)]
-        else:
-            src = wrows(owner, lo, size)
+        ref = piece(owner, step, way, kind)
+        i = ring_sem(step, way, kind)
         target = (up, s) if way == 0 else (down, s)
-        i = way * far + step - 1
-        return remote(src, wrows(owner, lo, size), ring_send.at[i], ring_recv.at[i], target)
-
-    def came(step, way):
-        owner = lax.rem(y + ny - step if way == 0 else y + step, ny)
-        if step < far:
-            lo, size = 0, half
-        else:
-            lo, size = (0, cut) if way == 0 else (cut, half - cut)
-        return wrows(owner, lo, size)
-
-    def to_sibling(step, way):
-        part = came(step, way)
-        return remote(part, part, sib_send, sib_recv, (y, sib))
-
-    def serve(step):
+        return remote(ref, ref, ring_send.at[i], ring_recv.at[i], target)
+
+    def source(step, way):
+        return lax.rem(y + ny - step if way == 0 else y + step, ny)
+
+    def serve(step, kind):
         for way in (0, 1):
-            part = came(step, way)
-            pltpu.make_async_copy(part, part, ring_recv.at[way * far + step - 1]).wait()
+            ref = piece(source(step, way), step, way, kind)
+            pltpu.make_async_copy(ref, ref, ring_recv.at[ring_sem(step, way, kind)]).wait()
             if step < far:
-                ring(step + 1, way).start()
-            to_sibling(step, way).start()
-
-    ring(1, 0).start()
-    ring(1, 1).start()
+                ring(step + 1, way, kind).start()
+            if kind == 1:
+                remote(ref, ref, sib_send, sib_recv, (y, sib)).start()
+            else:
+                for t in range(1, nx):
+                    to = lax.rem(x + t, nx)
+                    remote(
+                        ref,
+                        ref,
+                        share_send,
+                        share_recv.at[way * far + step - 1],
+                        (y, z * nq + to * NC + c),
+                    ).start()
+
+    def gather(step):
+        for way in (0, 1):
+            lo, size = span(step, way)
+            row = pl.ds(mo(source(step, way) * shard + c * half + lo, 16), size)
+            if nx > 1:
+                drain(wf.at[row, pl.ds(0, (nx - 1) * part)], share_recv.at[way * far + step - 1])
+            ref = wf.at[row, pl.ds(shared, shared)]
+            remote(ref, ref, sib_send, sib_recv, (y, sib)).start()
+
+    for kind in (0, 1):
+        for way in (0, 1):
+            ring(1, way, kind).start()
 
     def post(i, carry):
         hop = (i + 1) // 2
@@ -248,6 +297,7 @@
     )
     send_cot.start()
 
+    serve(1, 0)
     drain(posv.at[pl.ds(0, ns - 1)], pos_sem.at[1])
     all_pos = jnp.reshape(posv[...], (ns, tok))
     mine = (all_pos // rows) == s
@@ -259,6 +309,7 @@
     used = lax.dot_general(
         places[0], jnp.ones((total, 128), BF16), (((0,), (0,)), ((), ())), preferred_element_type=F32
     )
+    serve(1, 1)
     drain(arr.at[pl.ds(0, (ns - 1) * mr)], msg_sem.at[1])
     arr_t = jnp.transpose(arr[...])
     for f in range(4):
@@ -268,7 +319,8 @@
     )
     send_fr.start()
     if far > 1:
-        serve(1)
+        serve(2, 0)
+    gather(1)
     send_fr.wait_recv()
     wide = 2 * rows
     for j in range(2):
@@ -306,10 +358,14 @@
         ).start()
         return carry
 
-    lax.fori_loop(0, ny, stem, 0)
+    if far > 1:
+        lax.fori_loop(0, ny // 2, stem, 0)
+        serve(2, 1)
+        lax.fori_loop(ny // 2, ny, stem, 0)
+    else:
+        lax.fori_loop(0, ny, stem, 0)
     own_cot.wait()
     send_cot.wait_recv()
-    own_w.wait()
 
     def shard_at(offset):
         return lax.rem(y + ny + offset, ny)
@@ -324,8 +380,8 @@
                 lanes = slice(j * wide, (j + 1) * wide)
                 grad = gp[i * half : (i + 1) * half] * slope[pl.ds(l0, half), lanes]
                 gt[i * half : (i + 1) * half, lanes] = grad.astype(BF16)
-        part = lax.dot_general(xt[...], gt[...], NT, preferred_element_type=F32)
-        xsend[g * km : (g + 1) * km, :] = part.astype(BF16)
+        product = lax.dot_general(xt[...], gt[...], NT, preferred_element_type=F32)
+        xsend[g * km : (g + 1) * km, :] = product.astype(BF16)
         mine_x = pl.ds(mo((g * nx + x) * xr, 16), xr)
         xrecv[mine_x, :] = xsend[pl.ds(mo(g * km + x * xr, 16), xr), :]
 
@@ -386,18 +442,22 @@
             slot = (sum(len(h) for h in groups(ny)[:g]) + i) * zp
             ysend[slot : slot + zp, :] = turned[:, : ysend.shape[1]].astype(BF16)
             here = yrecv.at[pl.ds(mo((y * NC + c) * zp, 16), zp)]
-            piece = ysend.at[pl.ds(slot, zp)]
+            mine_y = ysend.at[pl.ds(slot, zp)]
             to = shard_at(o)
             if o == 0:
                 yrecv[pl.ds(mo((y * NC + c) * zp, 16), zp), :] = ysend[slot : slot + zp, :]
             else:
-                remote(piece, here, y_sem.at[0], y_sem.at[1], (to, s)).start()
-            remote(piece, here, y_sem.at[0], y_sem.at[1], (to, sib)).start()
+                remote(mine_y, here, y_sem.at[0], y_sem.at[1], (to, s)).start()
+            remote(mine_y, here, y_sem.at[0], y_sem.at[1], (to, sib)).start()
 
     for g, steps in enumerate(steps_of(ny)):
         for step in steps:
-            if step > 1 or (step == 1 and far == 1):
-                serve(step)
+            if step > 2:
+                serve(step, 0)
+                serve(step, 1)
+        for step in steps:
+            if step > 1:
+                gather(step)
         back(g)
         if g > 0:
             middle(g - 1)
@@ -449,8 +509,11 @@
 
     for way in (0, 1):
         for step in range(1, far + 1):
-            ring(step, way).wait_send()
+            for kind in (0, 1):
+                ring(step, way, kind).wait_send()
     drain(wf.at[pl.ds(0, (ny - 1) * half)], sib_send)
+    if nx > 1:
+        drain(wf.at[pl.ds(0, (ny - 1) * half), pl.ds(0, (nx - 1) * part)], share_send)
     drain(posv.at[pl.ds(0, ns - 1)], pos_sem.at[0])
     drain(arr.at[pl.ds(0, (ns - 1) * mr)], msg_sem.at[0])
     send_cot.wait_send()
@@ -483,7 +546,7 @@
     zp = -(-taps * NC * (mels // ns) // 16) * 16
     cw = jnp.transpose(conv_weight, (1, 0, 2)).reshape(km, ch)
     vmem = pl.BlockSpec(memory_space=pltpu.VMEM)
-    hbm = pl.BlockSpec(memory_space=pl.ANY)
+    hbm = pl.BlockSpec(memory_space=pltpu.HBM)
     total = 4 * rows
     dma = pltpu.SemaphoreType.DMA
     merged, gw = pl.pallas_call(
@@ -492,9 +555,14 @@
             jax.ShapeDtypeStruct((rows, feats), BF16),
             jax.ShapeDtypeStruct((taps, mels // ns, ch // ny), F32),
         ),
-        in_specs=[vmem, vmem, vmem, vmem, hbm, vmem, hbm],
+        in_specs=[hbm] * 7,
         out_specs=(hbm, vmem),
         scratch_shapes=[
+            pltpu.VMEM((frames, mels), BF16),
+            pltpu.VMEM((1, tok), I32),
+            pltpu.VMEM((km, ch), BF16),
+            pltpu.VMEM((ch,), F32),
+            pltpu.VMEM((1, feats), F32),
             pltpu.VMEM((ch, feats), BF16),
             pltpu.VMEM((2 * rows, feats), BF16),
             pltpu.VMEM((ch, km), BF16),
@@ -516,10 +584,12 @@
             pltpu.VMEM((ny * zp, lanes_y), BF16),
             pltpu.VMEM((ny * NC * zp, lanes_y), BF16),
             pltpu.VMEM((rows, feats), BF16),
-            dma((2 * far,)),
-            dma((2 * far,)),
+            dma((4 * far,)),
+            dma((4 * far,)),
             dma,
             dma,
+            dma,
+            dma((2 * far,)),
             dma((2,)),
             dma((2,)),
             dma((2,)),
@@ -530,10 +600,10 @@
             dma((n_groups,)),
             dma((n_groups,)),
             dma((2,)),
-            dma((2,)),
+            dma((7,)),
         ],
         compiler_params=pltpu.CompilerParams(
-            collective_id=0, has_side_effects=True, vmem_limit_bytes=48 << 20
+            collective_id=0, has_side_effects=True, vmem_limit_bytes=60 << 20
         ),
     )(
         mel_frames[0],

time: 76 us -> 72.5 us (0.954)
  local copies, waits for them, and re-layouts: 7.96 us -> 2.91 us
  Pallas kernels: 67 us -> 68.8 us
    unnamed x16 -> x4, local copies, waits for them, and re-layouts: 7.96 us -> 2.91 us
    pallas_call x1, Pallas kernels: 67 us -> 68.8 us  [body(): pl.pallas_call(functools.partial(kernel, ny, ns, nx), out_shape=(jax.Shap...]
where the time goes in v4:
time: 72.5 us; the launch traced here: 72.4 us
  Pallas kernels  68.8 us (95%)
  local copies, waits for them, and re-layouts  2.91 us (4%)
    pallas_call x1, Pallas kernels, body(): pl.pallas_call(functools.partial(kernel, ny, ns, nx), out_shape=(jax.Shap...  68.8 us
    unnamed x4, local copies, waits for them, and re-layouts  2.91 us

profile of v4, /device:TPU:1, one launch (start us, length us, event | category | flops | bytes accessed | tf_op | source)
XLA Modules:
  0.0 72.4 jit_solution(2698216383636648227)
XLA Ops:
  0.6 68.8 %shard_map.86 = (bf16[256,2048]{1,0:T(8,128)(2,1)}, f32[3,2,160]{2,1,0:T(2,128)}) custom-call(bf16[256,128]{1,0:T(8,128)(2,1)} %bitcast.11, s32[1,128]{1,0:T(1,128)} %pos_in.1, bf16[384,1280]{1,0:T(8,128)(2,1)} %bitcast.10, f32[1280]{0:T(1024)} %bias_in.1, bf16[160,2048]{1,0:T(8,128)(2,1)} %w_ref.1, f32[1,2048]{1,0:T(1,128)} %bitcast.12, ...), custom_call_target="tpu_custom_call" | custom-call | tf_op jit(solution)/shard_map/pallas_call | solution.py:552
  69.5 0.0 copy-start
  69.5 2.3 %copy.11 = bf16[1,256,2048]{2,1,0:T(8,128)(2,1)} copy(bf16[1,256,2048]{2,1,0:T(8,128)(2,1)} %bitcast.9) | data formatting | bytes 2097152
  71.8 0.0 copy-done
  71.8 0.6 copy.12
Async XLA Ops:
  69.5 2.3 %copy-start = (f32[3,2,160]{2,1,0:T(2,128)S(1)}, f32[3,2,160]{2,1,0:T(2,128)}, u32[]{:S(2)}) copy-start(f32[3,2,160]{2,1,0:T(2,128)} %get-tuple-element.5) | copy-start | bytes 11524

commit v5 on v4

--- a/solution.py
+++ b/solution.py
@@ -68,7 +68,6 @@
     zrecv,
     ysend,
     yrecv,
-    mscr,
     ring_send,
     ring_recv,
     sib_send,
@@ -231,10 +230,10 @@
         row = pl.ds(mo(owner * shard + c * half + lo, 16), size)
         if kind == 0:
             return wf.at[row, pl.ds(mo(shared + x * part, 128), part)]
-        return wf.at[row, pl.ds(0, shared)]
+        return wf.at[row, pl.ds((kind - 1) * (shared // 2), shared // 2)]
 
     def ring_sem(step, way, kind):
-        return (way * far + step - 1) * 2 + kind
+        return (way * far + step - 1) * 3 + kind
 
     def ring(step, way, kind):
         owner = lax.rem(y + ny + 1 - step if way == 0 else y + step - 1, ny)
@@ -252,7 +251,7 @@
             pltpu.make_async_copy(ref, ref, ring_recv.at[ring_sem(step, way, kind)]).wait()
             if step < far:
                 ring(step + 1, way, kind).start()
-            if kind == 1:
+            if kind:
                 remote(ref, ref, sib_send, sib_recv, (y, sib)).start()
             else:
                 for t in range(1, nx):
@@ -274,7 +273,7 @@
             ref = wf.at[row, pl.ds(shared, shared)]
             remote(ref, ref, sib_send, sib_recv, (y, sib)).start()
 
-    for kind in (0, 1):
+    for kind in (0, 1, 2):
         for way in (0, 1):
             ring(1, way, kind).start()
 
@@ -297,7 +296,12 @@
     )
     send_cot.start()
 
+    def serve_if(step, kind):
+        if step <= far:
+            serve(step, kind)
+
     serve(1, 0)
+    serve(1, 1)
     drain(posv.at[pl.ds(0, ns - 1)], pos_sem.at[1])
     all_pos = jnp.reshape(posv[...], (ns, tok))
     mine = (all_pos // rows) == s
@@ -309,7 +313,9 @@
     used = lax.dot_general(
         places[0], jnp.ones((total, 128), BF16), (((0,), (0,)), ((), ())), preferred_element_type=F32
     )
-    serve(1, 1)
+    serve(1, 2)
+    serve_if(2, 0)
+    serve_if(2, 1)
     drain(arr.at[pl.ds(0, (ns - 1) * mr)], msg_sem.at[1])
     arr_t = jnp.transpose(arr[...])
     for f in range(4):
@@ -318,9 +324,8 @@
         fr.at[:, pl.ds(0, rows)], fr.at[:, pl.ds(rows, rows)], fr_sem.at[0], fr_sem.at[1], (y, sib)
     )
     send_fr.start()
-    if far > 1:
-        serve(2, 0)
-    gather(1)
+    serve_if(2, 2)
+    serve_if(3, 0)
     send_fr.wait_recv()
     wide = 2 * rows
     for j in range(2):
@@ -358,12 +363,15 @@
         ).start()
         return carry
 
+    serve_if(3, 1)
+    gather(1)
+    serve_if(4, 0)
+    lax.fori_loop(0, ny // 2, stem, 0)
+    serve_if(3, 2)
     if far > 1:
-        lax.fori_loop(0, ny // 2, stem, 0)
-        serve(2, 1)
-        lax.fori_loop(ny // 2, ny, stem, 0)
-    else:
-        lax.fori_loop(0, ny, stem, 0)
+        gather(2)
+    lax.fori_loop(ny // 2, ny, stem, 0)
+    serve_if(4, 1)
     own_cot.wait()
     send_cot.wait_recv()
 
@@ -450,17 +458,16 @@
                 remote(mine_y, here, y_sem.at[0], y_sem.at[1], (to, s)).start()
             remote(mine_y, here, y_sem.at[0], y_sem.at[1], (to, sib)).start()
 
+    back(0)
+    serve_if(4, 2)
     for g, steps in enumerate(steps_of(ny)):
         for step in steps:
             if step > 2:
-                serve(step, 0)
-                serve(step, 1)
-        for step in steps:
-            if step > 1:
                 gather(step)
-        back(g)
         if g > 0:
-            middle(g - 1)
+            back(g)
+    for g in range(len(groups(ny)) - 1):
+        middle(g)
 
     drain(ptr, pt_sem.at[1])
     drain(wf.at[pl.ds(0, (ny - 1) * half)], sib_recv)
@@ -478,16 +485,15 @@
     def project(i, carry):
         lanes = pl.ds(mo(i * block_w, 128), block_w)
         out = jnp.dot(pooled_rows, wf[:, lanes], preferred_element_type=F32) + pbias_ref[:, lanes]
-        mscr[:, lanes] = jnp.where(keep, out, 0.0).astype(BF16)
+        merged_ref[:, lanes] = jnp.where(keep, out, 0.0).astype(BF16)
         return carry
 
     lax.fori_loop(0, feats // block_w, project, 0)
-    put = pltpu.make_async_copy(mscr, merged_ref, loc_sem.at[0])
-    put.start()
-
+
+    for g in range(len(groups(ny)) - 1):
+        last(g)
     middle(len(groups(ny)) - 1)
-    for g in range(len(groups(ny))):
-        last(g)
+    last(len(groups(ny)) - 1)
     drain(yrecv.at[pl.ds(0, (ny * NC - 1) * zp)], y_sem.at[1])
     sums = []
     for h in range(NC):
@@ -509,7 +515,7 @@
 
     for way in (0, 1):
         for step in range(1, far + 1):
-            for kind in (0, 1):
+            for kind in (0, 1, 2):
                 ring(step, way, kind).wait_send()
     drain(wf.at[pl.ds(0, (ny - 1) * half)], sib_send)
     if nx > 1:
@@ -525,7 +531,6 @@
         if nz > 1:
             drain(zrecv.at[pl.ds(0, (nz - 1) * zp)], z_send.at[g])
     drain(yrecv.at[pl.ds(0, (ny * NC - 1) * zp)], y_sem.at[0])
-    put.wait()
 
 
 def body(nx, mel_frames, positions, conv_weight, conv_bias, proj_weight, proj_bias, cotangent):
@@ -556,7 +561,7 @@
             jax.ShapeDtypeStruct((taps, mels // ns, ch // ny), F32),
         ),
         in_specs=[hbm] * 7,
-        out_specs=(hbm, vmem),
+        out_specs=(vmem, vmem),
         scratch_shapes=[
             pltpu.VMEM((frames, mels), BF16),
             pltpu.VMEM((1, tok), I32),
@@ -583,9 +588,8 @@
             pltpu.VMEM((n_groups * nz * zp, lanes_g), BF16),
             pltpu.VMEM((ny * zp, lanes_y), BF16),
             pltpu.VMEM((ny * NC * zp, lanes_y), BF16),
-            pltpu.VMEM((rows, feats), BF16),
-            dma((4 * far,)),
-            dma((4 * far,)),
+            dma((6 * far,)),
+            dma((6 * far,)),
             dma,
             dma,
             dma,

time: 72.5 us -> 70.2 us (0.968)
  Pallas kernels: 68.8 us -> 66.5 us
    pallas_call x1, Pallas kernels: 68.8 us -> 66.5 us  [body(): pl.pallas_call(functools.partial(kernel, ny, ns, nx), out_shape=(jax.Shap...]
where the time goes in v5:
time: 70.2 us; the launch traced here: 70.1 us
  Pallas kernels  66.5 us (95%)
  local copies, waits for them, and re-layouts  2.91 us (4%)
    pallas_call x1, Pallas kernels, body(): pl.pallas_call(functools.partial(kernel, ny, ns, nx), out_shape=(jax.Shap...  66.5 us
    unnamed x4, local copies, waits for them, and re-layouts  2.91 us

profile of v5, /device:TPU:1, one launch (start us, length us, event | category | flops | bytes accessed | tf_op | source)
XLA Modules:
  0.0 70.1 jit_solution(3985128154894240268)
XLA Ops:
  0.6 66.5 %shard_map.86 = (bf16[256,2048]{1,0:T(8,128)(2,1)}, f32[3,2,160]{2,1,0:T(2,128)}) custom-call(bf16[256,128]{1,0:T(8,128)(2,1)} %bitcast.11, s32[1,128]{1,0:T(1,128)} %pos_in.1, bf16[384,1280]{1,0:T(8,128)(2,1)} %bitcast.10, f32[1280]{0:T(1024)} %bias_in.1, bf16[160,2048]{1,0:T(8,128)(2,1)} %w_ref.1, f32[1,2048]{1,0:T(1,128)} %bitcast.12, ...), custom_call_target="tpu_custom_call" | custom-call | tf_op jit(solution)/shard_map/pallas_call | solution.py:557
  67.2 0.0 copy-start
  67.2 2.3 %copy.11 = bf16[1,256,2048]{2,1,0:T(8,128)(2,1)} copy(bf16[1,256,2048]{2,1,0:T(8,128)(2,1)} %bitcast.9) | data formatting | bytes 2097152
  69.5 0.0 copy-done
  69.5 0.6 copy.12
Async XLA Ops:
  67.2 2.3 %copy-start = (f32[3,2,160]{2,1,0:T(2,128)S(1)}, f32[3,2,160]{2,1,0:T(2,128)}, u32[]{:S(2)}) copy-start(f32[3,2,160]{2,1,0:T(2,128)} %get-tuple-element.5) | copy-start | bytes 11524

commit v6 on v5

--- a/solution.py
+++ b/solution.py
@@ -302,6 +302,9 @@
 
     serve(1, 0)
     serve(1, 1)
+    serve(1, 2)
+    serve_if(2, 0)
+    serve_if(2, 1)
     drain(posv.at[pl.ds(0, ns - 1)], pos_sem.at[1])
     all_pos = jnp.reshape(posv[...], (ns, tok))
     mine = (all_pos // rows) == s
@@ -313,9 +316,6 @@
     used = lax.dot_general(
         places[0], jnp.ones((total, 128), BF16), (((0,), (0,)), ((), ())), preferred_element_type=F32
     )
-    serve(1, 2)
-    serve_if(2, 0)
-    serve_if(2, 1)
     drain(arr.at[pl.ds(0, (ns - 1) * mr)], msg_sem.at[1])
     arr_t = jnp.transpose(arr[...])
     for f in range(4):
@@ -366,12 +366,13 @@
     serve_if(3, 1)
     gather(1)
     serve_if(4, 0)
-    lax.fori_loop(0, ny // 2, stem, 0)
+    lax.fori_loop(0, ny // 4, stem, 0)
     serve_if(3, 2)
     if far > 1:
         gather(2)
-    lax.fori_loop(ny // 2, ny, stem, 0)
+    lax.fori_loop(ny // 4, ny - ny // 4, stem, 0)
     serve_if(4, 1)
+    lax.fori_loop(ny - ny // 4, ny, stem, 0)
     own_cot.wait()
     send_cot.wait_recv()
 
@@ -488,11 +489,13 @@
         merged_ref[:, lanes] = jnp.where(keep, out, 0.0).astype(BF16)
         return carry
 
-    lax.fori_loop(0, feats // block_w, project, 0)
-
+    blocks = feats // block_w
+    lax.fori_loop(0, blocks // 2, project, 0)
+
+    middle(len(groups(ny)) - 1)
     for g in range(len(groups(ny)) - 1):
         last(g)
-    middle(len(groups(ny)) - 1)
+    lax.fori_loop(blocks // 2, blocks, project, 0)
     last(len(groups(ny)) - 1)
     drain(yrecv.at[pl.ds(0, (ny * NC - 1) * zp)], y_sem.at[1])
     sums = []
@@ -607,7 +610,7 @@
             dma((7,)),
         ],
         compiler_params=pltpu.CompilerParams(
-            collective_id=0, has_side_effects=True, vmem_limit_bytes=60 << 20
+            collective_id=0, has_side_effects=True, vmem_limit_bytes=44 << 20
         ),
     )(
         mel_frames[0],

time: 70.2 us -> 67.1 us (0.956)
  Pallas kernels: 66.5 us -> 58.1 us
  local copies, waits for them, and re-layouts: 2.91 us -> 7.96 us
    pallas_call x1, Pallas kernels: 66.5 us -> 58.1 us  [body(): pl.pallas_call(functools.partial(kernel, ny, ns, nx), out_shape=(jax.Shap...]
    unnamed x4 -> x16, local copies, waits for them, and re-layouts: 2.91 us -> 7.96 us
where the time goes in v6:
time: 67.1 us; the launch traced here: 66.7 us
  Pallas kernels  58.1 us (87%)
  local copies, waits for them, and re-layouts  7.96 us (12%)
    pallas_call x1, Pallas kernels, body(): pl.pallas_call(functools.partial(kernel, ny, ns, nx), out_shape=(jax.Shap...  58.1 us
    unnamed x16, local copies, waits for them, and re-layouts  7.96 us

profile of v6, /device:TPU:1, one launch (start us, length us, event | category | flops | bytes accessed | tf_op | source)
XLA Modules:
  0.0 66.7 jit_solution(14878513819652278622)
XLA Ops:
  0.6 0.0 copy-start.6
  0.6 0.6 copy-done.6
  1.3 0.0 copy-start
  1.3 1.2 %copy-done = bf16[1,256,2048]{2,1,0:T(8,128)(2,1)S(1)} copy-done((bf16[1,256,2048]{2,1,0:T(8,128)(2,1)S(1)}, bf16[1,256,2048]{2,1,0:T(8,128)(2,1)}, u32[]{:S(2)}) %copy-start) | copy-done | bytes 1048600
  2.5 0.0 copy-start.1
  2.5 1.2 %copy-done.1 = bf16[128,3,1280]{2,0,1:T(8,128)(2,1)S(1)} copy-done((bf16[128,3,1280]{2,0,1:T(8,128)(2,1)S(1)}, bf16[128,3,1280]{2,0,1:T(8,128)(2,1)}, u32[]{:S(2)}) %copy-start.1) | copy-done | bytes 983064
  3.7 0.0 copy-start.2
  3.7 1.1 %copy-done.2 = bf16[160,2048]{1,0:T(8,128)(2,1)S(1)} copy-done((bf16[160,2048]{1,0:T(8,128)(2,1)S(1)}, bf16[160,2048]{1,0:T(8,128)(2,1)}, u32[]{:S(2)}) %copy-start.2) | copy-done | bytes 655384
  4.8 0.0 copy-start.3
  4.8 0.8 %copy-done.3 = bf16[1,256,128]{2,1,0:T(8,128)(2,1)S(1)} copy-done((bf16[1,256,128]{2,1,0:T(8,128)(2,1)S(1)}, bf16[1,256,128]{2,1,0:T(8,128)(2,1)}, u32[]{:S(2)}) %copy-start.3) | copy-done | bytes 65560
  5.6 0.0 copy-start.4
  5.6 0.7 %copy-done.4 = f32[1280]{0:T(1024)S(1)} copy-done((f32[1280]{0:T(1024)S(1)}, f32[1280]{0:T(1024)}, u32[]{:S(2)}) %copy-start.4) | copy-done | bytes 5144
  6.3 0.0 copy-start.5
  6.3 0.7 %copy-done.5 = f32[2048]{0:T(1024)S(1)} copy-done((f32[2048]{0:T(1024)S(1)}, f32[2048]{0:T(1024)}, u32[]{:S(2)}) %copy-start.5) | copy-done | bytes 8216
  7.0 58.1 %shard_map.86 = (bf16[256,2048]{1,0:T(8,128)(2,1)S(1)}, f32[3,2,160]{2,1,0:T(2,128)S(1)}) custom-call(bf16[256,128]{1,0:T(8,128)(2,1)S(1)} %bitcast.11, s32[1,128]{1,0:T(1,128)S(1)} %copy-done.6, bf16[384,1280]{1,0:T(8,128)(2,1)S(1)} %bitcast.10, f32[1280]{0:T(1024)S(1)} %copy-done.4, bf16[160,2048]{1,0:T(8,128)(2,1)S(1)} %copy-done.2, ...), custom_call_target="tpu_custom_call" | custom-call | tf_op jit(solution)/shard_map/pallas_call | solution.py:560
  65.2 1.0 %copy.11 = bf16[1,256,2048]{2,1,0:T(8,128)(2,1)} copy(bf16[1,256,2048]{2,1,0:T(8,128)(2,1)S(1)} %bitcast.9) | data formatting | bytes 2097152
  66.2 0.6 copy.12
Async XLA Ops:
  0.6 0.7 copy-start.6
  1.3 1.2 %copy-start = (bf16[1,256,2048]{2,1,0:T(8,128)(2,1)S(1)}, bf16[1,256,2048]{2,1,0:T(8,128)(2,1)}, u32[]{:S(2)}) copy-start(bf16[1,256,2048]{2,1,0:T(8,128)(2,1)} %param.13) | copy-start | bytes 3145732
  2.5 1.2 %copy-start.1 = (bf16[128,3,1280]{2,0,1:T(8,128)(2,1)S(1)}, bf16[128,3,1280]{2,0,1:T(8,128)(2,1)}, u32[]{:S(2)}) copy-start(bf16[128,3,1280]{2,0,1:T(8,128)(2,1)} %param.9) | copy-start | bytes 2949124
  3.7 1.1 %copy-start.2 = (bf16[160,2048]{1,0:T(8,128)(2,1)S(1)}, bf16[160,2048]{1,0:T(8,128)(2,1)}, u32[]{:S(2)}) copy-start(bf16[160,2048]{1,0:T(8,128)(2,1)} %w_ref.1) | copy-start | bytes 1966084
  4.8 0.8 %copy-start.3 = (bf16[1,256,128]{2,1,0:T(8,128)(2,1)S(1)}, bf16[1,256,128]{2,1,0:T(8,128)(2,1)}, u32[]{:S(2)}) copy-start(bf16[1,256,128]{2,1,0:T(8,128)(2,1)} %param.7) | copy-start | bytes 196612
  5.6 0.7 %copy-start.4 = (f32[1280]{0:T(1024)S(1)}, f32[1280]{0:T(1024)}, u32[]{:S(2)}) copy-start(f32[1280]{0:T(1024)} %bias_in.1) | copy-start | bytes 15364
  6.3 0.7 %copy-start.5 = (f32[2048]{0:T(1024)S(1)}, f32[2048]{0:T(1024)}, u32[]{:S(2)}) copy-start(f32[2048]{0:T(1024)} %param.12) | copy-start | bytes 24580

commit v7 on v6

--- a/solution.py
+++ b/solution.py
@@ -610,7 +610,7 @@
             dma((7,)),
         ],
         compiler_params=pltpu.CompilerParams(
-            collective_id=0, has_side_effects=True, vmem_limit_bytes=44 << 20
+            collective_id=0, has_side_effects=True, vmem_limit_bytes=60 << 20
         ),
     )(
         mel_frames[0],

time: 67.1 us -> 62.9 us (0.937)
  local copies, waits for them, and re-layouts: 7.96 us -> 2.91 us
  Pallas kernels: 58.1 us -> 59.2 us
    unnamed x16 -> x4, local copies, waits for them, and re-layouts: 7.96 us -> 2.91 us
    pallas_call x1, Pallas kernels: 58.1 us -> 59.2 us  [body(): pl.pallas_call(functools.partial(kernel, ny, ns, nx), out_shape=(jax.Shap...]
where the time goes in v7:
time: 62.9 us; the launch traced here: 62.8 us
  Pallas kernels  59.2 us (94%)
  local copies, waits for them, and re-layouts  2.91 us (5%)
  between operations  0.65 us (1%)
    pallas_call x1, Pallas kernels, body(): pl.pallas_call(functools.partial(kernel, ny, ns, nx), out_shape=(jax.Shap...  59.2 us
    unnamed x4, local copies, waits for them, and re-layouts  2.91 us

profile of v7, /device:TPU:1, one launch (start us, length us, event | category | flops | bytes accessed | tf_op | source)
XLA Modules:
  0.0 62.8 jit_solution(5967621282233155497)
XLA Ops:
  0.6 59.2 %shard_map.86 = (bf16[256,2048]{1,0:T(8,128)(2,1)}, f32[3,2,160]{2,1,0:T(2,128)}) custom-call(bf16[256,128]{1,0:T(8,128)(2,1)} %bitcast.11, s32[1,128]{1,0:T(1,128)} %pos_in.1, bf16[384,1280]{1,0:T(8,128)(2,1)} %bitcast.10, f32[1280]{0:T(1024)} %bias_in.1, bf16[160,2048]{1,0:T(8,128)(2,1)} %w_ref.1, f32[1,2048]{1,0:T(1,128)} %bitcast.12, ...), custom_call_target="tpu_custom_call" | custom-call | tf_op jit(solution)/shard_map/pallas_call | solution.py:560
  59.9 0.0 copy-start
  59.9 2.3 %copy.11 = bf16[1,256,2048]{2,1,0:T(8,128)(2,1)} copy(bf16[1,256,2048]{2,1,0:T(8,128)(2,1)} %bitcast.9) | data formatting | bytes 2097152
  62.2 0.0 copy-done
  62.2 0.6 copy.12
Async XLA Ops:
  59.9 2.3 %copy-start = (f32[3,2,160]{2,1,0:T(2,128)S(1)}, f32[3,2,160]{2,1,0:T(2,128)}, u32[]{:S(2)}) copy-start(f32[3,2,160]{2,1,0:T(2,128)} %get-tuple-element.5) | copy-start | bytes 11524

commit v8 on v7

--- a/solution.py
+++ b/solution.py
@@ -395,7 +395,9 @@
         xrecv[mine_x, :] = xsend[pl.ds(mo(g * km + x * xr, 16), xr), :]
 
         def pass_x(t, carry):
-            to = lax.rem(x + t, nx)
+            back_t = nx - t
+            hop = (back_t + 1) // 2
+            to = lax.rem(x + nx + hop * (2 * lax.rem(back_t, 2) - 1), nx)
             remote(
                 xsend.at[pl.ds(mo(g * km + to * xr, 16), xr)],
                 xrecv.at[mine_x],
@@ -427,8 +429,9 @@
         zrecv[mine_z, :] = zsend[mine_z, :]
 
         def pass_z(t, carry):
-            hop = (t + 1) // 2
-            to = lax.rem(z + nz + hop * (2 * lax.rem(t, 2) - 1), nz)
+            back_t = nz - t
+            hop = (back_t + 1) // 2
+            to = lax.rem(z + nz + hop * (2 * lax.rem(back_t, 2) - 1), nz)
             remote(
                 zsend.at[pl.ds(mo((g * nz + to) * zp, 16), zp)],
                 zrecv.at[mine_z],

time: 62.9 us -> 62.6 us (level)
  no operation moved by 1% of the time
where the time goes in v8:
time: 62.6 us; the launch traced here: 62.4 us
  Pallas kernels  58.9 us (94%)
  local copies, waits for them, and re-layouts  2.91 us (5%)
  between operations  0.65 us (1%)
    pallas_call x1, Pallas kernels, body(): pl.pallas_call(functools.partial(kernel, ny, ns, nx), out_shape=(jax.Shap...  58.9 us
    unnamed x4, local copies, waits for them, and re-layouts  2.91 us

profile of v8, /device:TPU:1, one launch (start us, length us, event | category | flops | bytes accessed | tf_op | source)
XLA Modules:
  0.0 62.4 jit_solution(246457595008359450)
XLA Ops:
  0.6 58.9 %shard_map.86 = (bf16[256,2048]{1,0:T(8,128)(2,1)}, f32[3,2,160]{2,1,0:T(2,128)}) custom-call(bf16[256,128]{1,0:T(8,128)(2,1)} %bitcast.11, s32[1,128]{1,0:T(1,128)} %pos_in.1, bf16[384,1280]{1,0:T(8,128)(2,1)} %bitcast.10, f32[1280]{0:T(1024)} %bias_in.1, bf16[160,2048]{1,0:T(8,128)(2,1)} %w_ref.1, f32[1,2048]{1,0:T(1,128)} %bitcast.12, ...), custom_call_target="tpu_custom_call" | custom-call | tf_op jit(solution)/shard_map/pallas_call | solution.py:563
  59.5 0.0 copy-start
  59.5 2.3 %copy.11 = bf16[1,256,2048]{2,1,0:T(8,128)(2,1)} copy(bf16[1,256,2048]{2,1,0:T(8,128)(2,1)} %bitcast.9) | data formatting | bytes 2097152
  61.8 0.0 copy-done
  61.9 0.6 copy.12
Async XLA Ops:
  59.5 2.3 %copy-start = (f32[3,2,160]{2,1,0:T(2,128)S(1)}, f32[3,2,160]{2,1,0:T(2,128)}, u32[]{:S(2)}) copy-start(f32[3,2,160]{2,1,0:T(2,128)} %get-tuple-element.5) | copy-start | bytes 11524
